TPU v7x, 768 devices: a whole 4x8x12 slice. The times are simulated.
768 devices in a mesh: ta: 16 (over y, core), ha: 48 (over x, z).
Axes of the slice: x: 4, y: 8, z: 12, core: 2. Of those that a mesh axis runs over, the one named last changes fastest.
Arguments:
- query_states: bfloat16 [32, 96, 56, 768], P('ta', 'ha'), may hold values from -51 to 51
- key_states: bfloat16 [32, 96, 56, 768], P('ta', 'ha'), may hold values from -6 to 6
- value_states: bfloat16 [32, 96, 56, 768], P('ta', 'ha'), may hold values from -6 to 6
- conv_weight: bfloat16 [27, 768], replicated, may hold values from -1.1953125 to 1.1953125
- out_grad: bfloat16 [32, 96, 56, 768], P('ta', 'ha'), may hold values from -6 to 6
- tile_mask: int32 [16, 48, 9], replicated, may hold values from 0 to 1, as said below
- clip_lengths: int32 [32], replicated, may hold values from 2 to 56
Outputs:
- layer_out: bfloat16 [32, 96, 56, 768], P('ta', 'ha')
- query_grad: bfloat16 [32, 96, 56, 768], P('ta', 'ha')
- key_grad: bfloat16 [32, 96, 56, 768], P('ta', 'ha')
- value_grad: bfloat16 [32, 96, 56, 768], P('ta', 'ha')
Inputs may be any that keep to these rules, and one draw needn't show every extreme that they name: `tile_mask`: entries are 0 or 1; entry 4, a tile's own keys, is always 1.
All inputs are finite; a program needn't handle non-finite values.
Results may differ from a plain program's by a relative error of at most 0.0095.
Values may be sent and summed in bfloat16 or wider, within the bound.
A program may use at most 128 MiB of HBM per device.

v0:
```python
import jax
import jax.numpy as jnp
from jax import lax
from jax.sharding import PartitionSpec as P

HEAD_DIM = 128


CONTRACT_LAST = (((1,), (1,)), ((), ()))
CONTRACT_FIRST = (((0,), (0,)), ((), ()))


def from_behind(x, axis, by):
    devices = lax.axis_size(axis)
    pairs = [(i, i + by) for i in range(devices) if 0 <= i + by < devices]
    return lax.ppermute(x, axis, pairs)


def padded(cells, sides, width):
    for axis, dim in sides:
        count = lax.axis_size(axis)
        ends = count - 1
        head = lax.slice_in_dim(cells, 0, width, axis=dim)
        tail = lax.slice_in_dim(cells, cells.shape[dim] - width, cells.shape[dim], axis=dim)
        cells = jnp.concatenate(
            [
                lax.ppermute(tail, axis, [(i, (i + 1) % count) for i in range(ends)]),
                cells,
                lax.ppermute(head, axis, [((i + 1) % count, i) for i in range(ends)]),
            ],
            axis=dim,
        )
    return cells


def depthwise(source, weight, size_t, size_h, width_len):
    result = jnp.zeros((size_t, size_h, width_len, source.shape[3]), jnp.float32)
    for offset_id in range(27):
        step_t, step_h, step_w = (offset_id // 9, offset_id // 3 % 3, offset_id % 3)
        piece = source[
            step_t : step_t + size_t, step_h : step_h + size_h, step_w : step_w + width_len
        ].astype(jnp.float32)
        result = result + weight[offset_id].astype(jnp.float32) * piece
    return result


def window_valid(tile_mask, clip_lengths, index_t, index_h, count_t, count_h, tile_side, width_len):
    tile_offset = jnp.arange(3 * tile_side) // tile_side
    frame_ids = index_t * tile_side - tile_side + jnp.arange(3 * tile_side)
    in_time = (frame_ids >= 0) & (frame_ids < count_t * tile_side)
    frame_lens = jnp.where(
        in_time, clip_lengths[jnp.clip(frame_ids, 0, count_t * tile_side - 1)], 0
    )
    height_ids = index_h + tile_offset - 1
    in_height = (height_ids >= 0) & (height_ids < count_h)
    entries = tile_mask[index_t, index_h].reshape(3, 3)
    kept_tiles = entries[tile_offset][:, tile_offset] == 1
    columns = jnp.arange(width_len)
    key_valid = (
        kept_tiles[:, :, None]
        & in_height[None, :, None]
        & (columns[None, None, :] < frame_lens[:, None, None])
    )
    return key_valid.reshape(-1)


def return_partials(partials, tile_side):
    upper_part = partials[:, :tile_side]
    middle = partials[:, tile_side : 2 * tile_side]
    lower_part = partials[:, 2 * tile_side :]
    for direction, piece_grad in ((-1, upper_part), (1, lower_part)):
        middle = middle + from_behind(piece_grad.astype(jnp.bfloat16), "ta", direction).astype(
            jnp.float32
        )
    left_part = middle[:, :, :tile_side]
    centre = middle[:, :, tile_side : 2 * tile_side]
    right_part = middle[:, :, 2 * tile_side :]
    for direction, piece_grad in ((-1, left_part), (1, right_part)):
        centre = centre + from_behind(piece_grad.astype(jnp.bfloat16), "ha", direction).astype(
            jnp.float32
        )
    return centre


def head_cols(matrix, head_id):
    return lax.dynamic_slice_in_dim(matrix, head_id * HEAD_DIM, HEAD_DIM, 1)


def heads_to_rows(stacked):
    return stacked.transpose(1, 0, 2).reshape(stacked.shape[1], -1)


def shards(query_states, key_states, value_states, conv_weight, out_grad, tile_mask, clip_lengths):
    tile_side, tile_other, width_len, channels = query_states.shape
    head_count = channels // HEAD_DIM
    score_scale = HEAD_DIM ** (-0.5)
    index_t = lax.axis_index("ta")
    index_h = lax.axis_index("ha")
    count_t = lax.axis_size("ta")
    count_h = lax.axis_size("ha")
    queries = tile_side * tile_side * width_len
    window_len = 3 * tile_side
    tile_shape = (tile_side, tile_side, width_len, channels)
    window_shape = (window_len, window_len, width_len, channels)
    window = padded(jnp.stack([key_states, value_states]), (("ta", 1), ("ha", 2)), tile_side)
    key_window = window[0]
    value_window = window[1]
    key_valid = window_valid(
        tile_mask, clip_lengths, index_t, index_h, count_t, count_h, tile_side, width_len
    )
    query_flat = query_states.reshape(queries, channels)
    grad_flat = out_grad.reshape(queries, channels)
    key_flat = key_window.reshape(-1, channels)
    value_flat = value_window.reshape(-1, channels)

    def forward_head(head_id):
        query_head = head_cols(query_flat, head_id)
        grad_head = head_cols(grad_flat, head_id)
        key_head = head_cols(key_flat, head_id)
        value_head = head_cols(value_flat, head_id)
        scores = (
            lax.dot_general(query_head, key_head, CONTRACT_LAST, preferred_element_type=jnp.float32)
            * score_scale
        )
        scores = jnp.where(key_valid[None, :], scores, -jnp.inf)
        row_max = jnp.max(scores, axis=-1, keepdims=True)
        exponent = jnp.exp(scores - row_max)
        row_total = jnp.sum(exponent, axis=-1, keepdims=True)
        softmax_p = exponent / row_total
        probs_bf = softmax_p.astype(jnp.bfloat16)
        attention = jnp.dot(probs_bf, value_head, preferred_element_type=jnp.float32)
        row_delta = jnp.sum(grad_head.astype(jnp.float32) * attention, axis=-1)
        dprobs = lax.dot_general(
            grad_head, value_head, CONTRACT_LAST, preferred_element_type=jnp.float32
        )
        dscores = (softmax_p * (dprobs - row_delta[:, None])).astype(jnp.bfloat16)
        query_part = jnp.dot(dscores, key_head, preferred_element_type=jnp.float32) * score_scale
        log_total = row_max[:, 0] + jnp.log(row_total[:, 0])
        key_part = (
            lax.dot_general(dscores, query_head, CONTRACT_FIRST, preferred_element_type=jnp.float32)
            * score_scale
        )
        value_part = lax.dot_general(
            probs_bf, grad_head, CONTRACT_FIRST, preferred_element_type=jnp.float32
        )
        return (attention, query_part, log_total, row_delta, key_part, value_part)

    attention_h, query_h, total_h, delta_h, key_h, value_h = lax.map(
        forward_head, jnp.arange(head_count, dtype=jnp.int32)
    )
    attention = heads_to_rows(attention_h)
    value_slab = value_window[tile_side - 1 : 2 * tile_side + 1, tile_side - 1 : 2 * tile_side + 1]
    value_slab = jnp.pad(value_slab, ((0, 0), (0, 0), (1, 1), (0, 0)))
    conv_out = depthwise(value_slab, conv_weight, tile_side, tile_side, width_len)
    layer_out = (attention.reshape(tile_shape) + conv_out).astype(jnp.bfloat16)
    query_grad = heads_to_rows(query_h).reshape(tile_shape).astype(jnp.bfloat16)
    key_part = heads_to_rows(key_h)
    value_part = heads_to_rows(value_h)
    value_padded = jnp.pad(value_part.reshape(window_shape), ((0, 0), (0, 0), (1, 1), (0, 0)))
    grad_full = out_grad.astype(jnp.float32)
    for offset_id in range(27):
        step_t, step_h, step_w = (offset_id // 9, offset_id // 3 % 3, offset_id % 3)
        first_t = tile_side - 1 + step_t
        first_h = tile_side - 1 + step_h
        value_padded = value_padded.at[
            first_t : first_t + tile_side,
            first_h : first_h + tile_side,
            step_w : step_w + width_len,
        ].add(conv_weight[offset_id].astype(jnp.float32) * grad_full)
    value_part = value_padded[:, :, 1 : width_len + 1]
    partials = jnp.stack([key_part.reshape(window_shape), value_part])
    owned_grads = return_partials(partials, tile_side)
    key_grad = owned_grads[0].astype(jnp.bfloat16)
    value_grad = owned_grads[1].astype(jnp.bfloat16)
    return (layer_out, query_grad, key_grad, value_grad)


def solution(mesh):
    placed = (
        P("ta", "ha", None, None),
        P("ta", "ha", None, None),
        P("ta", "ha", None, None),
        P(),
        P("ta", "ha", None, None),
        P(),
        P(),
    )
    return jax.shard_map(
        shards,
        mesh=mesh,
        in_specs=placed,
        out_specs=(
            P("ta", "ha", None, None),
            P("ta", "ha", None, None),
            P("ta", "ha", None, None),
            P("ta", "ha", None, None),
        ),
        check_vma=False,
    )
```

profile of v0, /device:TPU:26, one launch (start us, length us, event | category | flops | bytes accessed | tf_op | source)
XLA Modules:
  0.0 397.1 jit_solution(9815444093859607040)
XLA Ops:
  3.8 3.6 collective-permute-start.1
  7.5 6.7 %collective-permute-done = bf16[2,2,2,56,768]{4,3,2,1,0:T(8,128)(2,1)S(1)} collective-permute-done((bf16[2,2,2,56,768]{4,3,2,1,0:T(8,128)(2,1)S(1)}, bf16[2,2,2,56,768]{4,3,2,1,0:T(8,128)(2,1)S(1)}, u32[]{:S(2)}, u32[]{:S(2)}) %collective-permute-start) | collective-permute-done | bytes 688160 | tf_op jit(solution)/shard_map/ppermute | solution.py:27
  15.9 2.6 pad_maximum_fusion.2
  18.6 4.3 %collective-permute-start.2 = (bf16[2,6,2,56,768]{4,3,2,1,0:T(8,128)(2,1)}, bf16[2,6,2,56,768]{4,3,2,1,0:T(8,128)(2,1)}, u32[]{:S(2)}, u32[]{:S(2)}) collective-permute-start(bf16[2,6,2,56,768]{4,3,2,1,0:T(8,128)(2,1)} %pad_maximum_fusion.2), channel_id=1, source_target_pairs={{0,1},{1,2},{2,3},{3,4},{4,5},{5,6},{6,7},{7,8},{8,9},{9,10},{10,1... | collective-permute-start | bytes 6193160 | tf_op jit(solution)/shard_map/ppermute | solution.py:27
  22.8 12.2 %collective-permute-start.3 = (bf16[2,6,2,56,768]{4,3,2,1,0:T(8,128)(2,1)}, bf16[2,6,2,56,768]{4,3,2,1,0:T(8,128)(2,1)}, u32[]{:S(2)}, u32[]{:S(2)}) collective-permute-start(bf16[2,6,2,56,768]{4,3,2,1,0:T(8,128)(2,1)} %pad_maximum_fusion.2), channel_id=1, source_target_pairs={{1,0},{2,1},{3,2},{4,3},{5,4},{6,5},{7,6},{8,7},{9,8},{10,9},{11,1... | collective-permute-start | bytes 6193160 | tf_op jit(solution)/shard_map/ppermute | solution.py:29
  39.9 35.7 %collective-permute-done.2 = bf16[2,6,2,56,768]{4,3,2,1,0:T(8,128)(2,1)} collective-permute-done((bf16[2,6,2,56,768]{4,3,2,1,0:T(8,128)(2,1)}, bf16[2,6,2,56,768]{4,3,2,1,0:T(8,128)(2,1)}, u32[]{:S(2)}, u32[]{:S(2)}) %collective-permute-start.2) | collective-permute-done | bytes 2064416 | tf_op jit(solution)/shard_map/ppermute | solution.py:27
  77.3 3.2 pad_maximum_fusion.1
  80.5 3.3 slice_bitcast_fusion.3
  84.4 81.6 %while.44 = (s32[]{:T(128)}, f32[6,224,128]{2,1,0:T(8,128)}, bf16[6,224,128]{2,1,0:T(8,128)(2,1)}, f32[6,2016,128]{2,1,0:T(8,128)}, f32[6,2016,128]{2,1,0:T(8,12...) while((s32[]{:T(128)}, f32[6,224,128]{2,1,0:T(8,128)}, ...), condition=%wide.region_4.5_spmd.clone, body=%wide.region_0.4_spmd.clone.sunk | while | flops 701232448 | bytes 16710735 | solution.py:148
  94.6 2.4 fusion.110
  121.8 2.3 fusion.110
  135.4 2.3 fusion.110
  149.0 2.4 fusion.110
  162.6 2.3 fusion.110
  166.0 10.7 %copy.22 = f32[2016,6,128]{2,1,0:T(8,128)} copy(f32[2016,6,128]{2,0,1:T(8,128)} %bitcast.91) | data formatting | bytes 12386304 | tf_op jit(solution)/shard_map/transpose | solution.py:90
  176.7 8.9 %reshape_reshape.8 = f32[6,6,56,768]{3,2,1,0:T(8,128)} reshape(f32[2016,6,128]{2,1,0:T(8,128)} %copy.22) | data formatting | bytes 12386304 | tf_op jit(solution)/shard_map/reshape;reshape | solution.py:159
  185.6 3.5 pad.117
  189.3 2.9 copy-done.3
  192.3 3.3 scatter-add.91
  196.9 3.3 scatter-add.94
  203.6 3.3 scatter-add.96
  208.2 3.3 scatter-add.99
  214.9 3.3 scatter-add.101
  219.5 3.3 scatter-add.104
  226.1 3.3 scatter-add.106
  230.7 3.3 scatter-add.109
  237.4 3.4 scatter-add.111
  242.0 3.4 scatter-add.114
  248.6 3.3 scatter-add.116
  253.2 3.3 scatter-add.119
  259.9 3.4 scatter-add.121
  264.5 3.4 scatter-add.124
  271.2 3.3 scatter-add.126
  275.8 3.3 scatter-add.129
  282.4 3.3 scatter-add.131
  287.0 3.5 scatter-add.134
  290.5 6.4 %slice_bitcast_fusion = f32[1,6,6,56,768]{4,3,2,1,0:T(8,128)} fusion(f32[6,6,58,768]{3,2,1,0:T(8,128)} %scatter-add.134), kind=kLoop, calls=%fused_computation.44 | loop fusion | bytes 12386304 | tf_op jit(solution)/shard_map/stack | solution.py:171
  296.9 12.6 %copy.21 = f32[2016,6,128]{2,1,0:T(8,128)} copy(f32[2016,6,128]{2,0,1:T(8,128)S(1)} %bitcast.90) | data formatting | bytes 12386304 | tf_op jit(solution)/shard_map/transpose | solution.py:90
  309.5 9.0 %stack_reshape_reshape.3 = f32[1,6,6,56,768]{4,3,2,1,0:T(8,128)} reshape(f32[2016,6,128]{2,1,0:T(8,128)} %copy.21) | data formatting | bytes 12386304 | tf_op jit(solution)/shard_map/stack;reshape;reshape | solution.py:171
  318.5 8.2 %fusion.31 = bf16[2,6,6,56,768]{4,3,2,1,0:T(8,128)(2,1)} fusion(f32[1,6,6,56,768]{4,3,2,1,0:T(8,128)} %slice_bitcast_fusion, f32[1,6,6,56,768]{4,3,2,1,0:T(8,128)} %stack_reshape_reshape.3), kind=kLoop, calls=%fused_computation.43 | loop fusion | flops 3096576 | bytes 18579456 | tf_op jit(solution)/shard_map/convert.32
  326.8 2.6 fusion.80
  329.4 5.6 %collective-permute-start.4 = (bf16[2,2,6,56,768]{4,3,2,1,0:T(8,128)(2,1)S(1)}, bf16[2,2,6,56,768]{4,3,2,1,0:T(8,128)(2,1)S(1)}, u32[]{:S(2)}, u32[]{:S(2)}) collective-permute-start(bf16[2,2,6,56,768]{4,3,2,1,0:T(8,128)(2,1)S(1)} %get-tuple-element.501), channel_id=1, source_target_pairs={{48,0},{96,48},{144,96},{192,144},{240,192},{288,240},{336,288},{3... | collective-permute-start | bytes 6193160 | tf_op jit(solution)/shard_map/ppermute | solution.py:16
  337.3 20.9 %collective-permute-done.4 = bf16[2,2,6,56,768]{4,3,2,1,0:T(8,128)(2,1)S(1)} collective-permute-done((bf16[2,2,6,56,768]{4,3,2,1,0:T(8,128)(2,1)S(1)}, bf16[2,2,6,56,768]{4,3,2,1,0:T(8,128)(2,1)S(1)}, u32[]{:S(2)}, u32[]{:S(2)}) %collective-permute-start.4) | collective-permute-done | bytes 2064416 | tf_op jit(solution)/shard_map/ppermute | solution.py:16
  358.2 4.0 collective-permute-done.5
  362.2 2.7 fusion.77
  366.0 6.3 %collective-permute-start.6 = (bf16[2,2,2,56,768]{4,3,2,1,0:T(8,128)(2,1)}, bf16[2,2,2,56,768]{4,3,2,1,0:T(8,128)(2,1)}, u32[]{:S(2)}, u32[]{:S(2)}) collective-permute-start(bf16[2,2,2,56,768]{4,3,2,1,0:T(8,128)(2,1)} %get-tuple-element.506), channel_id=1, source_target_pairs={{1,0},{2,1},{3,2},{4,3},{5,4},{6,5},{7,6},{8,7},{9,8},{10,9},{11,1... | collective-permute-start | bytes 2064392 | tf_op jit(solution)/shard_map/ppermute | solution.py:16
  382.2 6.7 %add_convert_fusion = bf16[2,2,56,768]{3,2,1,0:T(8,128)(2,1)} fusion(f32[2,2,56,768]{3,2,1,0:T(8,128)} %reshape_reshape.7, bf16[6,6,56,768]{3,2,1,0:T(8,128)(2,1)S(1)} %copy-done.5, f32[768]{0:T(1024)S(1)} %get-tuple-element.469, f32[768]{0:T(1024)S(1)} %get-tuple-element.470, f32[768]{0:T(1024)S(1)} %get-tuple-element.445, f32[768]{0:T(1024)} %copy-done.11, ...), kind=kLoop, calls=%fused_computation.117 | loop fusion | flops 14106624 | bytes 5587968 | tf_op jit(solution)/shard_map/convert_element_type | solution.py:155
  388.8 5.4 %collective-permute-done.7 = bf16[2,2,2,56,768]{4,3,2,1,0:T(8,128)(2,1)} collective-permute-done((bf16[2,2,2,56,768]{4,3,2,1,0:T(8,128)(2,1)}, bf16[2,2,2,56,768]{4,3,2,1,0:T(8,128)(2,1)}, u32[]{:S(2)}, u32[]{:S(2)}) %collective-permute-start.7) | collective-permute-done | bytes 688160 | tf_op jit(solution)/shard_map/ppermute | solution.py:16
  (213 shorter events, 131.6 us)
Async XLA Ops:
  0.6 34.5 %copy-start = (s32[16,48,9]{1,0,2:T(8,128)S(1)}, s32[16,48,9]{1,0,2:T(8,128)}, u32[]{:S(2)}) copy-start(s32[16,48,9]{1,0,2:T(8,128)} %param.68) | copy-start | bytes 82948
  0.6 76.6 %copy-start.7 = (bf16[2,2,56,768]{3,2,1,0:T(8,128)(2,1)S(1)}, bf16[2,2,56,768]{3,2,1,0:T(8,128)(2,1)}, u32[]{:S(2)}) copy-start(bf16[2,2,56,768]{3,2,1,0:T(8,128)(2,1)} %param.64) | copy-start | bytes 1032196
  0.7 76.6 %copy-start.6 = (bf16[2,2,56,768]{3,2,1,0:T(8,128)(2,1)S(1)}, bf16[2,2,56,768]{3,2,1,0:T(8,128)(2,1)}, u32[]{:S(2)}) copy-start(bf16[2,2,56,768]{3,2,1,0:T(8,128)(2,1)} %param.65) | copy-start | bytes 1032196
  0.7 37.6 %copy-start.10 = (bf16[27,768]{1,0:T(8,128)(2,1)S(1)}, bf16[27,768]{1,0:T(8,128)(2,1)}, u32[]{:S(2)}) copy-start(bf16[27,768]{1,0:T(8,128)(2,1)} %param.66) | copy-start | bytes 124420
  1.9 12.3 %collective-permute-start = (bf16[2,2,2,56,768]{4,3,2,1,0:T(8,128)(2,1)S(1)}, bf16[2,2,2,56,768]{4,3,2,1,0:T(8,128)(2,1)S(1)}, u32[]{:S(2)}, u32[]{:S(2)}) collective-permute-start(bf16[2,2,2,56,768]{4,3,2,1,0:T(8,128)(2,1)S(1)} %pad_maximum_fusion.3), channel_id=1, source_target_pairs={{0,48},{48,96},{96,144},{144,192},{192,240},{240,288},{288,336},{3... | collective-permute-start | bytes 2064392 | tf_op jit(solution)/shard_map/ppermute | solution.py:27
  3.8 12.1 %collective-permute-start.1 = (bf16[2,2,2,56,768]{4,3,2,1,0:T(8,128)(2,1)S(1)}, bf16[2,2,2,56,768]{4,3,2,1,0:T(8,128)(2,1)S(1)}, u32[]{:S(2)}, u32[]{:S(2)}) collective-permute-start(bf16[2,2,2,56,768]{4,3,2,1,0:T(8,128)(2,1)S(1)} %pad_maximum_fusion.3), channel_id=1, source_target_pairs={{48,0},{96,48},{144,96},{192,144},{240,192},{288,240},{336,288},{3... | collective-permute-start | bytes 2064392 | tf_op jit(solution)/shard_map/ppermute | solution.py:29
  18.6 57.0 %collective-permute-start.2 = (bf16[2,6,2,56,768]{4,3,2,1,0:T(8,128)(2,1)}, bf16[2,6,2,56,768]{4,3,2,1,0:T(8,128)(2,1)}, u32[]{:S(2)}, u32[]{:S(2)}) collective-permute-start(bf16[2,6,2,56,768]{4,3,2,1,0:T(8,128)(2,1)} %pad_maximum_fusion.2), channel_id=1, source_target_pairs={{0,1},{1,2},{2,3},{3,4},{4,5},{5,6},{6,7},{7,8},{8,9},{9,10},{10,1... | collective-permute-start | bytes 6193160 | tf_op jit(solution)/shard_map/ppermute | solution.py:27
  22.8 54.4 %collective-permute-start.3 = (bf16[2,6,2,56,768]{4,3,2,1,0:T(8,128)(2,1)}, bf16[2,6,2,56,768]{4,3,2,1,0:T(8,128)(2,1)}, u32[]{:S(2)}, u32[]{:S(2)}) collective-permute-start(bf16[2,6,2,56,768]{4,3,2,1,0:T(8,128)(2,1)} %pad_maximum_fusion.2), channel_id=1, source_target_pairs={{1,0},{2,1},{3,2},{4,3},{5,4},{6,5},{7,6},{8,7},{9,8},{10,9},{11,1... | collective-permute-start | bytes 6193160 | tf_op jit(solution)/shard_map/ppermute | solution.py:29
  39.1 183.7 %copy-start.25 = (f32[768]{0:T(1024)}, f32[768]{0:T(1024)S(1)}, u32[]{:S(2)}) copy-start(f32[768]{0:T(1024)S(1)} %get-tuple-element.460) | copy-start | bytes 9220
  39.1 185.7 %copy-start.24 = (f32[768]{0:T(1024)}, f32[768]{0:T(1024)S(1)}, u32[]{:S(2)}) copy-start(f32[768]{0:T(1024)S(1)} %get-tuple-element.459) | copy-start | bytes 9220
  39.1 190.3 %copy-start.23 = (f32[768]{0:T(1024)}, f32[768]{0:T(1024)S(1)}, u32[]{:S(2)}) copy-start(f32[768]{0:T(1024)S(1)} %get-tuple-element.458) | copy-start | bytes 9220
  39.1 194.9 %copy-start.22 = (f32[768]{0:T(1024)}, f32[768]{0:T(1024)S(1)}, u32[]{:S(2)}) copy-start(f32[768]{0:T(1024)S(1)} %get-tuple-element.457) | copy-start | bytes 9220
  39.1 196.9 %copy-start.21 = (f32[768]{0:T(1024)}, f32[768]{0:T(1024)S(1)}, u32[]{:S(2)}) copy-start(f32[768]{0:T(1024)S(1)} %get-tuple-element.456) | copy-start | bytes 9220
  39.1 201.6 %copy-start.20 = (f32[768]{0:T(1024)}, f32[768]{0:T(1024)S(1)}, u32[]{:S(2)}) copy-start(f32[768]{0:T(1024)S(1)} %get-tuple-element.455) | copy-start | bytes 9220
  39.2 206.2 %copy-start.19 = (f32[768]{0:T(1024)}, f32[768]{0:T(1024)S(1)}, u32[]{:S(2)}) copy-start(f32[768]{0:T(1024)S(1)} %get-tuple-element.454) | copy-start | bytes 9220
  39.2 208.2 %copy-start.18 = (f32[768]{0:T(1024)}, f32[768]{0:T(1024)S(1)}, u32[]{:S(2)}) copy-start(f32[768]{0:T(1024)S(1)} %get-tuple-element.453) | copy-start | bytes 9220
  39.2 212.8 %copy-start.17 = (f32[768]{0:T(1024)}, f32[768]{0:T(1024)S(1)}, u32[]{:S(2)}) copy-start(f32[768]{0:T(1024)S(1)} %get-tuple-element.452) | copy-start | bytes 9220
  39.2 217.4 %copy-start.16 = (f32[768]{0:T(1024)}, f32[768]{0:T(1024)S(1)}, u32[]{:S(2)}) copy-start(f32[768]{0:T(1024)S(1)} %get-tuple-element.451) | copy-start | bytes 9220
  39.2 219.4 %copy-start.15 = (f32[768]{0:T(1024)}, f32[768]{0:T(1024)S(1)}, u32[]{:S(2)}) copy-start(f32[768]{0:T(1024)S(1)} %get-tuple-element.450) | copy-start | bytes 9220
  39.2 224.0 %copy-start.14 = (f32[768]{0:T(1024)}, f32[768]{0:T(1024)S(1)}, u32[]{:S(2)}) copy-start(f32[768]{0:T(1024)S(1)} %get-tuple-element.449) | copy-start | bytes 9220
  39.2 228.7 %copy-start.13 = (f32[768]{0:T(1024)}, f32[768]{0:T(1024)S(1)}, u32[]{:S(2)}) copy-start(f32[768]{0:T(1024)S(1)} %get-tuple-element.448) | copy-start | bytes 9220
  39.2 230.7 %copy-start.12 = (f32[768]{0:T(1024)}, f32[768]{0:T(1024)S(1)}, u32[]{:S(2)}) copy-start(f32[768]{0:T(1024)S(1)} %get-tuple-element.447) | copy-start | bytes 9220
  39.2 235.3 %copy-start.11 = (f32[768]{0:T(1024)}, f32[768]{0:T(1024)S(1)}, u32[]{:S(2)}) copy-start(f32[768]{0:T(1024)S(1)} %get-tuple-element.446) | copy-start | bytes 9220
  80.5 3.9 copy-start.2
  84.4 2.0 copy-start.28
  92.9 5.2 %copy-start.29 = (pred[6,6]{1,0:T(8,128)(4,1)S(1)}, pred[6,6]{1,0:T(8,128)(4,1)}, u32[]{:S(2)}) copy-start(pred[6,6]{1,0:T(8,128)(4,1)} %copy-done.28) | copy-start | bytes 112 | tf_op jit(solution)/shard_map/while
  106.5 5.1 %copy-start.29 = (pred[6,6]{1,0:T(8,128)(4,1)S(1)}, pred[6,6]{1,0:T(8,128)(4,1)}, u32[]{:S(2)}) copy-start(pred[6,6]{1,0:T(8,128)(4,1)} %copy-done.28) | copy-start | bytes 112 | tf_op jit(solution)/shard_map/while
  120.1 5.1 %copy-start.29 = (pred[6,6]{1,0:T(8,128)(4,1)S(1)}, pred[6,6]{1,0:T(8,128)(4,1)}, u32[]{:S(2)}) copy-start(pred[6,6]{1,0:T(8,128)(4,1)} %copy-done.28) | copy-start | bytes 112 | tf_op jit(solution)/shard_map/while
  125.2 2.0 copy-start.28
  133.7 5.1 %copy-start.29 = (pred[6,6]{1,0:T(8,128)(4,1)S(1)}, pred[6,6]{1,0:T(8,128)(4,1)}, u32[]{:S(2)}) copy-start(pred[6,6]{1,0:T(8,128)(4,1)} %copy-done.28) | copy-start | bytes 112 | tf_op jit(solution)/shard_map/while
  147.3 5.2 %copy-start.29 = (pred[6,6]{1,0:T(8,128)(4,1)S(1)}, pred[6,6]{1,0:T(8,128)(4,1)}, u32[]{:S(2)}) copy-start(pred[6,6]{1,0:T(8,128)(4,1)} %copy-done.28) | copy-start | bytes 112 | tf_op jit(solution)/shard_map/while
  160.9 5.1 %copy-start.29 = (pred[6,6]{1,0:T(8,128)(4,1)S(1)}, pred[6,6]{1,0:T(8,128)(4,1)}, u32[]{:S(2)}) copy-start(pred[6,6]{1,0:T(8,128)(4,1)} %copy-done.28) | copy-start | bytes 112 | tf_op jit(solution)/shard_map/while
  189.3 2.9 copy-start.3
  195.7 17.9 %copy-start.27 = (f32[768]{0:T(1024)S(1)}, f32[768]{0:T(1024)}, u32[]{:S(2)}) copy-start(f32[768]{0:T(1024)} %get-tuple-element.462) | copy-start | bytes 9220
  200.3 17.9 %copy-start.26 = (f32[768]{0:T(1024)S(1)}, f32[768]{0:T(1024)}, u32[]{:S(2)}) copy-start(f32[768]{0:T(1024)} %get-tuple-element.461) | copy-start | bytes 9220
  287.0 9.9 %slice-start.2 = ((s8[6193152]{0:T(1024)(128)(4,1)}), s8[1998848]{0:T(1024)(128)(4,1)S(1)}, s32[]{:S(2)}) async-start(s8[6193152]{0:T(1024)(128)(4,1)} %bitcast.88), calls=%async_computation.2 | async-start | bytes 3997696
  290.5 6.4 %slice-start.3 = ((s8[6193152]{0:T(1024)(128)(4,1)}), s8[4194304]{0:T(1024)(128)(4,1)S(1)}, s32[]{:S(2)}) async-start(s8[6193152]{0:T(1024)(128)(4,1)} %bitcast.88), calls=%async_computation.3 | async-start | bytes 8388608
  309.5 52.6 %slice-start = ((s8[6193152]{0:T(1024)(128)(4,1)}), s8[1998848]{0:T(1024)(128)(4,1)S(1)}, s32[]{:S(2)}) async-start(s8[6193152]{0:T(1024)(128)(4,1)} %bitcast.85), calls=%async_computation | async-start | bytes 3997696
  318.5 43.6 %slice-start.1 = ((s8[6193152]{0:T(1024)(128)(4,1)}), s8[4194304]{0:T(1024)(128)(4,1)S(1)}, s32[]{:S(2)}) async-start(s8[6193152]{0:T(1024)(128)(4,1)} %bitcast.85), calls=%async_computation.1 | async-start | bytes 8388608
  326.8 35.4 %copy-start.4 = (f32[1,6,6,56,768]{4,3,2,1,0:T(8,128)S(1)}, f32[1,6,6,56,768]{4,3,2,1,0:T(8,128)}, u32[]{:S(2)}) copy-start(f32[1,6,6,56,768]{4,3,2,1,0:T(8,128)} %stack_reshape_reshape.3) | copy-start | bytes 18579460
  329.4 28.8 %collective-permute-start.4 = (bf16[2,2,6,56,768]{4,3,2,1,0:T(8,128)(2,1)S(1)}, bf16[2,2,6,56,768]{4,3,2,1,0:T(8,128)(2,1)S(1)}, u32[]{:S(2)}, u32[]{:S(2)}) collective-permute-start(bf16[2,2,6,56,768]{4,3,2,1,0:T(8,128)(2,1)S(1)} %get-tuple-element.501), channel_id=1, source_target_pairs={{48,0},{96,48},{144,96},{192,144},{240,192},{288,240},{336,288},{3... | collective-permute-start | bytes 6193160 | tf_op jit(solution)/shard_map/ppermute | solution.py:16
  335.0 39.3 %copy-start.8 = (f32[6,224,128]{2,1,0:T(8,128)S(1)}, f32[6,224,128]{2,1,0:T(8,128)}, u32[]{:S(2)}) copy-start(f32[6,224,128]{2,1,0:T(8,128)} %get-tuple-element.388) | copy-start | bytes 2064388
  335.0 27.1 %collective-permute-start.5 = (bf16[2,2,6,56,768]{4,3,2,1,0:T(8,128)(2,1)S(1)}, bf16[2,2,6,56,768]{4,3,2,1,0:T(8,128)(2,1)S(1)}, u32[]{:S(2)}, u32[]{:S(2)}) collective-permute-start(bf16[2,2,6,56,768]{4,3,2,1,0:T(8,128)(2,1)S(1)} %get-tuple-element.502), channel_id=1, source_target_pairs={{0,48},{48,96},{96,144},{144,192},{192,240},{240,288},{288,336},{3... | collective-permute-start | bytes 6193160 | tf_op jit(solution)/shard_map/ppermute | solution.py:16
  364.8 13.0 %copy-start.5 = (bf16[6,6,56,768]{3,2,1,0:T(8,128)(2,1)S(1)}, bf16[6,6,56,768]{3,2,1,0:T(8,128)(2,1)}, u32[]{:S(2)}) copy-start(bf16[6,6,56,768]{3,2,1,0:T(8,128)(2,1)} %get-tuple-element.503) | copy-start | bytes 9289732
  364.8 14.2 %copy-start.9 = (bf16[6,224,128]{2,1,0:T(8,128)(2,1)S(1)}, bf16[6,224,128]{2,1,0:T(8,128)(2,1)}, u32[]{:S(2)}) copy-start(bf16[6,224,128]{2,1,0:T(8,128)(2,1)} %get-tuple-element.389) | copy-start | bytes 1032196
  366.0 22.8 %collective-permute-start.6 = (bf16[2,2,2,56,768]{4,3,2,1,0:T(8,128)(2,1)}, bf16[2,2,2,56,768]{4,3,2,1,0:T(8,128)(2,1)}, u32[]{:S(2)}, u32[]{:S(2)}) collective-permute-start(bf16[2,2,2,56,768]{4,3,2,1,0:T(8,128)(2,1)} %get-tuple-element.506), channel_id=1, source_target_pairs={{1,0},{2,1},{3,2},{4,3},{5,4},{6,5},{7,6},{8,7},{9,8},{10,9},{11,1... | collective-permute-start | bytes 2064392 | tf_op jit(solution)/shard_map/ppermute | solution.py:16
  372.3 21.9 %collective-permute-start.7 = (bf16[2,2,2,56,768]{4,3,2,1,0:T(8,128)(2,1)}, bf16[2,2,2,56,768]{4,3,2,1,0:T(8,128)(2,1)}, u32[]{:S(2)}, u32[]{:S(2)}) collective-permute-start(bf16[2,2,2,56,768]{4,3,2,1,0:T(8,128)(2,1)} %get-tuple-element.507), channel_id=1, source_target_pairs={{0,1},{1,2},{2,3},{3,4},{4,5},{5,6},{6,7},{7,8},{8,9},{9,10},{10,1... | collective-permute-start | bytes 2064392 | tf_op jit(solution)/shard_map/ppermute | solution.py:16
  377.9 19.2 %copy-start.1 = (s32[16,48,9]{1,0,2:T(8,128)S(1)}, s32[16,48,9]{1,0,2:T(8,128)}, u32[]{:S(2)}) copy-start(s32[16,48,9]{1,0,2:T(8,128)} %param.68) | copy-start | bytes 82948
  (4 other events, 8.1 us)
where the time goes:
time: 402 us; the launch traced here: 397 us
  local copies, waits for them, and re-layouts  143 us (36%)
  waiting for transfers between devices  76.1 us (19%)
  other arithmetic  73.9 us (18%)
  matrix products  61.1 us (15%)
  starting transfers between devices  38.1 us (9%)
  loops' own time  4.26 us (1%)
    scatter-add x18, local copies, waits for them, and re-layouts, shards(): value_padded = value_padded.at[first_t:first_t + tile_side, first_h:first...  60.3 us
    ppermute x2, waiting for transfers between devices, padded(): lax.ppermute(tail, axis, [(i, (i + 1) % count) for i in range(ends)])  42.3 us
    ppermute x4, waiting for transfers between devices, from_behind(): return lax.ppermute(x, axis, pairs)  30.2 us
    transpose x3, local copies, waits for them, and re-layouts, heads_to_rows(): return stacked.transpose(1, 0, 2).reshape(stacked.shape[1], -1)  24.7 us
    add x18, other arithmetic, shards(): value_padded = value_padded.at[first_t:first_t + tile_side, first_h:first...  21.5 us
    scatter-add x9, other arithmetic, shards(): value_padded = value_padded.at[first_t:first_t + tile_side, first_h:first...  16.5 us
    ppermute x4, starting transfers between devices, from_behind(): return lax.ppermute(x, axis, pairs)  16.1 us
    ppermute x2, starting transfers between devices, padded(): lax.ppermute(head, axis, [((i + 1) % count, i) for i in range(ends)])  15.8 us
  transfers between devices with their start and end apart: 8, of which 7 were waited for; matrix products, arithmetic and copies ran while one was open for 5% of the time, Pallas kernels for 0%

commit v1 on v0

v1 whole, which is shorter than its diff:
```python
import functools
import math

import jax
import jax.numpy as jnp
from jax import lax
from jax.experimental import pallas as pl
from jax.experimental.pallas import tpu as pltpu
from jax.sharding import PartitionSpec as P

MESH = pl.DeviceIdType.MESH
HEAD_DIM = 128
TILE_SIDE = 2
F32 = jnp.float32
BF16 = jnp.bfloat16
BIG = 1e30
LOG2E = math.log2(math.e)

AK, AV, AQ, AG = 0, 1, 2, 3
OWN, L, R, PP, PL_, PR, OO, OL, OR = range(9)

LAST = (((1,), (1,)), ((), ()))


def nt(a, b):
    return lax.dot_general(a, b, LAST, preferred_element_type=F32)


def nn(a, b):
    return jnp.dot(a, b, preferred_element_type=F32)


def kernel(
    heads, cells, rows, padded, n_t, n_h, chunks,
    q_hbm, k_hbm, v_hbm, w_hbm, g_hbm, mask_hbm, clip_hbm,
    out_hbm, dq_hbm, dk_hbm, dv_hbm,
    tiles, probs, dprobs, slot_max, top, total, attn, delta, key_acc, value_acc, staged,
    bias, penalty, stat_mat, stat_out, stat_in, w_ref, wf_ref, mask_ref, clip_ref,
    load_sem, aux_sem, store_sem, send_sem, recv_sem, stat_send, stat_recv,
):
    scale = HEAD_DIM ** -0.5
    c2 = scale * LOG2E
    t = lax.axis_index("ta")
    h = lax.axis_index("ha")
    parity = lax.rem(t, 2)
    a_p = 1 - 2 * parity
    a_rows = (0, a_p, -a_p)
    b_cols = (0, -1, 1)
    t_rows = tuple(lax.rem(t + a + n_t, n_t) for a in a_rows)
    h_cols = tuple(lax.rem(h + b + n_h, n_h) for b in b_cols)
    flip = (0, 2, 1)
    hpc = heads // chunks

    def load(arr, hd):
        src = (k_hbm, v_hbm, q_hbm, g_hbm)[arr]
        return pltpu.make_async_copy(
            src.at[:, pl.ds(hd * HEAD_DIM, HEAD_DIM)],
            tiles.at[arr, OWN, hd, pl.ds(0, rows)],
            load_sem.at[arr, hd],
        )

    for arr in (AK, AV, AQ, AG):
        for hd in range(heads):
            load(arr, hd).start()
    aux = (
        pltpu.make_async_copy(mask_hbm, mask_ref, aux_sem.at[0]),
        pltpu.make_async_copy(clip_hbm, clip_ref, aux_sem.at[1]),
        pltpu.make_async_copy(w_hbm, w_ref, aux_sem.at[2]),
    )
    for copy in aux:
        copy.start()

    barrier = pltpu.get_barrier_semaphore()
    for slot in range(1, 9):
        pl.semaphore_signal(
            barrier, inc=1, device_id=(t_rows[slot // 3], h_cols[slot % 3]), device_id_type=MESH
        )
    pl.semaphore_wait(barrier, 8)

    def travel(arr, src_slot, to, chunk):
        row, col = src_slot // 3, src_slot % 3
        if to in (L, R):
            dst_slot = 3 * row + flip[to]
            device = (t, h_cols[to])
        else:
            dst_slot = to + col
            device = (t_rows[to // 3], h)
        part = (pl.ds(chunk * hpc, hpc), pl.ds(0, rows))
        return pltpu.make_async_remote_copy(
            src_ref=tiles.at[(arr, src_slot) + part],
            dst_ref=tiles.at[(arr, dst_slot) + part],
            send_sem=send_sem.at[arr, dst_slot, chunk],
            recv_sem=recv_sem.at[arr, dst_slot, chunk],
            device_id=device,
            device_id_type=MESH,
        )

    sent = []

    def send(arr, src_slot, targets):
        for chunk in range(chunks):
            send_chunk(arr, src_slot, targets, chunk)

    def send_chunk(arr, src_slot, targets, chunk):
        for to in targets:
            copy = travel(arr, src_slot, to, chunk)
            copy.start()
            sent.append(copy)

    def arrived_chunk(arr, slot, chunk):
        part = (pl.ds(chunk * hpc, hpc), pl.ds(0, rows))
        place = tiles.at[(arr, slot) + part]
        pltpu.make_async_remote_copy(
            src_ref=place, dst_ref=place,
            send_sem=send_sem.at[arr, slot, chunk], recv_sem=recv_sem.at[arr, slot, chunk],
            device_id=(t, h_cols[1]), device_id_type=MESH,
        ).wait_recv()

    def arrived(arr, slot):
        for chunk in range(chunks):
            arrived_chunk(arr, slot, chunk)

    for arr, targets in ((AK, (OO, L, R, PP)), (AV, (OO, L, R, PP)), (AQ, (L, R, PP)), (AG, (L, R, PP))):
        for hd in range(heads):
            load(arr, hd).wait()
        send(arr, OWN, targets)

    @pl.loop(0, 4 * 9)
    def _(i):
        tiles[i // 9, i % 9, :, pl.ds(rows, padded - rows), :] = jnp.zeros(
            (heads, padded - rows, HEAD_DIM), BF16
        )

    @pl.loop(0, heads)
    def _(hd):
        zero = jnp.zeros((rows, HEAD_DIM), F32)
        top[hd] = zero - BIG
        total[hd] = zero
        attn[hd] = zero
        key_acc[hd] = zero
        value_acc[hd] = zero

    for copy in aux:
        copy.wait()

    lane = lax.broadcasted_iota(jnp.int32, (1, padded), 1)
    tile_frame = (lane >= 2 * cells).astype(jnp.int32)
    column = lane - cells * (
        (lane >= cells).astype(jnp.int32) + tile_frame + (lane >= 3 * cells).astype(jnp.int32)
    )
    shape = mask_ref.shape[1:]
    it = lax.broadcasted_iota(jnp.int32, shape, 0)
    ih = lax.broadcasted_iota(jnp.int32, shape, 1)

    def frame_len(frame):
        live = clip_ref[jnp.clip(frame, 0, TILE_SIDE * n_t - 1)]
        return jnp.where((frame >= 0) & (frame < TILE_SIDE * n_t), live, 0)

    def entry(index, at_t, at_h):
        here = (it == at_t) & (ih == at_h)
        picked = jnp.where(here, mask_ref[index], 0).astype(F32)
        return jnp.sum(picked, axis=(0, 1), keepdims=True)

    for slot in range(9):
        a, b = a_rows[slot // 3], b_cols[slot % 3]
        index = 3 * (a + 1) + (b + 1)
        first = TILE_SIDE * (t + a)
        len_0, len_1 = frame_len(first), frame_len(first + 1)
        inside = ((h + b >= 0) & (h + b < n_h)).astype(jnp.int32)
        live = jnp.where(tile_frame == 1, len_1 * inside, len_0 * inside)
        seen = (column < live) & (lane < rows)
        keep = jnp.where(seen, entry(index, t, h), 0.0)
        bias[slot] = jnp.where(keep > 0.5, 0.0, -BIG)
        facing = entry(8 - index, t + a, h + b)
        penalty[slot] = jnp.where((lane < rows), jnp.where(facing > 0.5, 0.0, BIG), BIG)

    def forward_slot(slot):
        @pl.loop(0, heads)
        def _(hd):
            q = tiles[AQ, OWN, hd, pl.ds(0, rows), :]
            g = tiles[AG, OWN, hd, pl.ds(0, rows), :]
            k = tiles[AK, slot, hd]
            v = tiles[AV, slot, hd]
            s = nt(q, k) + bias[slot]
            m = jnp.max(s, axis=-1, keepdims=True)
            p = jnp.exp2((s - m) * c2)
            row_sum = jnp.sum(p, axis=-1, keepdims=True)
            p_bf = p.astype(BF16)
            probs[slot, hd] = p_bf
            part = nn(p_bf, v)
            dprobs[slot, hd] = nt(g, v)
            m = jnp.broadcast_to(m, (rows, HEAD_DIM))
            slot_max[slot, hd] = m
            old = top[hd]
            new = jnp.maximum(old, m)
            keep_old = jnp.exp2((old - new) * c2)
            keep_new = jnp.exp2((m - new) * c2)
            top[hd] = new
            total[hd] = total[hd] * keep_old + row_sum * keep_new
            attn[hd] = attn[hd] * keep_old + part * keep_new

    def key_slot(slot):
        @pl.loop(0, heads)
        def _(hd):
            k = tiles[AK, OWN, hd, pl.ds(0, rows), :]
            v = tiles[AV, OWN, hd, pl.ds(0, rows), :]
            q = tiles[AQ, slot, hd]
            g = tiles[AG, slot, hd]
            log_total = stat_in[slot, 2 * hd] + penalty[slot]
            p = jnp.exp2(nt(k, q) * c2 - log_total)
            value_acc[hd] += nn(p.astype(BF16), g)
            ds = p * (nt(v, g) - stat_in[slot, 2 * hd + 1])
            key_acc[hd] += nn(ds.astype(BF16), q)

    def convolve(arr, hd, flipped):
        r_minus, r_plus = 2 - parity, 1 + parity
        in_t = ((t > 0).astype(F32), None, None, (t < n_t - 1).astype(F32))
        in_h = ((h > 0).astype(F32), None, None, (h < n_h - 1).astype(F32))
        source = {}
        for big_i in range(4):
            row = (r_minus, 0, 0, r_plus)[big_i]
            for big_j in range(4):
                col = (1, 0, 0, 2)[big_j]
                i, j = (1, 0, 1, 0)[big_i], (1, 0, 1, 0)[big_j]
                whole = tiles[arr, 3 * row + col, hd, pl.ds(0, rows), :].astype(F32)
                start = (2 * i + j) * cells
                piece = whole[start:start + cells]
                for factor in (in_t[big_i], in_h[big_j]):
                    if factor is not None:
                        piece = piece * factor
                source[big_i, big_j] = piece
        place = lax.broadcasted_iota(jnp.int32, (cells, HEAD_DIM), 0)
        pieces = []
        for i in range(2):
            for j in range(2):
                sums = []
                for dw in range(3):
                    acc = None
                    for dt in range(3):
                        for dh in range(3):
                            o = 9 * dt + 3 * dh + dw
                            o = 26 - o if flipped else o
                            term = source[i + dt, j + dh] * wf_ref[hd, pl.ds(o, 1), :]
                            acc = term if acc is None else acc + term
                    sums.append(acc)
                before = jnp.where(place == 0, 0.0, pltpu.roll(sums[0], 1, 0))
                after = jnp.where(place == cells - 1, 0.0, pltpu.roll(sums[2], cells - 1, 0))
                pieces.append(sums[1] + before + after)
        return pieces

    def store(which, hd):
        dst = (out_hbm, dq_hbm, dk_hbm, dv_hbm)[which]
        return pltpu.make_async_copy(
            staged.at[which, hd],
            dst.at[:, pl.ds(hd * HEAD_DIM, HEAD_DIM)],
            store_sem.at[which, hd],
        )

    def store_all(which):
        for hd in range(heads):
            store(which, hd).start()

    for hd in range(heads):
        wf_ref[hd] = w_ref[:, hd * HEAD_DIM:(hd + 1) * HEAD_DIM].astype(F32)

    forward_slot(OWN)
    arrived(AK, PP)
    arrived(AV, PP)
    forward_slot(PP)
    for chunk in range(chunks):
        for side in (L, R):
            arrived_chunk(AK, side, chunk)
            send_chunk(AK, side, (OO, PP), chunk)
    arrived(AK, OO)
    arrived(AV, OO)
    forward_slot(OO)
    for chunk in range(chunks):
        for side in (L, R):
            arrived_chunk(AV, side, chunk)
            send_chunk(AV, side, (OO, PP), chunk)
    send(AG, OWN, (OO,))
    forward_slot(L)
    forward_slot(R)
    for slot in (PL_, PR, OL, OR):
        arrived(AK, slot)
        arrived(AV, slot)
        forward_slot(slot)

    stat_mat[...] = jnp.zeros_like(stat_mat)

    @pl.loop(0, heads)
    def _(hd):
        g = tiles[AG, OWN, hd, pl.ds(0, rows), :].astype(F32)
        sums = total[hd]
        inverse = 1.0 / sums
        d = jnp.sum(g * attn[hd], axis=-1, keepdims=True) * inverse
        delta[hd] = d
        log_total = top[hd] * c2 + jnp.log(sums) * LOG2E
        lanes = lax.broadcasted_iota(jnp.int32, (rows, HEAD_DIM), 1)
        stat_mat[pl.ds(0, rows), :] = jnp.where(
            lanes == 2 * hd, log_total, jnp.where(lanes == 2 * hd + 1, d, stat_mat[pl.ds(0, rows), :])
        )

    as_rows = stat_mat[...].T
    for i in range(2 * heads):
        stat_out[i] = as_rows[i:i + 1]
        stat_in[OWN, i] = as_rows[i:i + 1]

    def stat_travel(slot):
        row, col = slot // 3, slot % 3
        dst_slot = 3 * row + flip[col]
        return pltpu.make_async_remote_copy(
            src_ref=stat_out,
            dst_ref=stat_in.at[dst_slot],
            send_sem=stat_send.at[dst_slot],
            recv_sem=stat_recv.at[dst_slot],
            device_id=(t_rows[row], h_cols[col]),
            device_id_type=MESH,
        )

    def stat_arrived(slot):
        pltpu.make_async_remote_copy(
            src_ref=stat_in.at[slot], dst_ref=stat_in.at[slot],
            send_sem=stat_send.at[slot], recv_sem=stat_recv.at[slot],
            device_id=(t, h_cols[1]), device_id_type=MESH,
        ).wait_recv()

    for slot in (PP, L, R, OO, PL_, PR, OL, OR):
        stat_travel(slot).start()

    send(AQ, OWN, (OO,))
    for side in (L, R):
        for chunk in range(chunks):
            arrived_chunk(AQ, side, chunk)
            send_chunk(AQ, side, (OO, PP), chunk)
    for chunk in range(chunks):
        arrived_chunk(AG, OO, chunk)
        send_chunk(AG, OO, (L, R), chunk)

    @pl.loop(0, heads)
    def _(hd):
        d = delta[hd]
        d = jnp.concatenate([d, d], axis=1)
        best = top[hd]

        def step(slot, acc):
            ds = probs[slot, hd].astype(F32) * (dprobs[slot, hd] - d)
            part = nn(ds.astype(BF16), tiles[AK, slot, hd])
            return acc + part * jnp.exp2((slot_max[slot, hd] - best) * c2)

        acc = lax.fori_loop(0, 9, step, jnp.zeros((rows, HEAD_DIM), F32))
        staged[1, hd] = (acc * (scale / total[hd])).astype(BF16)

    store_all(1)
    for side in (L, R):
        for chunk in range(chunks):
            arrived_chunk(AG, side, chunk)
            send_chunk(AG, side, (PP,), chunk)

    @pl.loop(0, heads)
    def _(hd):
        pieces = convolve(AV, hd, False)
        whole = jnp.concatenate(pieces, axis=0)
        staged[0, hd] = (attn[hd] / total[hd] + whole).astype(BF16)

    store_all(0)

    key_slot(OWN)
    for slot in (PP, L, R, PL_, PR, OO, OL, OR):
        stat_arrived(slot)
        if slot not in (L, R):
            arrived(AQ, slot)
            if slot != OO:
                arrived(AG, slot)
        key_slot(slot)

    place = lax.broadcasted_iota(jnp.int32, (rows, HEAD_DIM), 0)
    frame = (place >= 2 * cells).astype(jnp.int32)
    column = place - cells * (
        (place >= cells).astype(jnp.int32) + frame + (place >= 3 * cells).astype(jnp.int32)
    )
    own_0, own_1 = frame_len(TILE_SIDE * t), frame_len(TILE_SIDE * t + 1)
    live = column < jnp.where(frame == 1, own_1, own_0)

    @pl.loop(0, heads)
    def _(hd):
        whole = jnp.concatenate(convolve(AG, hd, True), axis=0)
        staged[2, hd] = jnp.where(live, key_acc[hd] * scale, 0.0).astype(BF16)
        staged[3, hd] = (jnp.where(live, value_acc[hd], 0.0) + whole).astype(BF16)

    store_all(2)
    store_all(3)
    for copy in sent:
        copy.wait_send()
    for slot in range(1, 9):
        stat_travel(slot).wait_send()
    for which in range(4):
        for hd in range(heads):
            store(which, hd).wait()


def shards(query_states, key_states, value_states, conv_weight, out_grad, tile_mask, clip_lengths):
    side_t, side_h, cells, channels = query_states.shape
    rows = side_t * side_h * cells
    padded = -(-rows // 128) * 128
    heads = channels // HEAD_DIM
    chunks = 2
    n_t, n_h = lax.axis_size("ta"), lax.axis_size("ha")
    flat = (rows, channels)
    any_space = pl.BlockSpec(memory_space=pl.ANY)
    outs = pl.pallas_call(
        functools.partial(kernel, heads, cells, rows, padded, n_t, n_h, chunks),
        out_shape=[jax.ShapeDtypeStruct(flat, BF16)] * 4,
        in_specs=[any_space] * 7,
        out_specs=[any_space] * 4,
        scratch_shapes=[
            pltpu.VMEM((4, 9, heads, padded, HEAD_DIM), BF16),
            pltpu.VMEM((9, heads, rows, padded), BF16),
            pltpu.VMEM((9, heads, rows, padded), F32),
            pltpu.VMEM((9, heads, rows, HEAD_DIM), F32),
            pltpu.VMEM((heads, rows, HEAD_DIM), F32),
            pltpu.VMEM((heads, rows, HEAD_DIM), F32),
            pltpu.VMEM((heads, rows, HEAD_DIM), F32),
            pltpu.VMEM((heads, rows, HEAD_DIM), F32),
            pltpu.VMEM((heads, rows, HEAD_DIM), F32),
            pltpu.VMEM((heads, rows, HEAD_DIM), F32),
            pltpu.VMEM((4, heads, rows, HEAD_DIM), BF16),
            pltpu.VMEM((9, 1, padded), F32),
            pltpu.VMEM((9, 1, padded), F32),
            pltpu.VMEM((padded, HEAD_DIM), F32),
            pltpu.VMEM((2 * heads, 1, padded), F32),
            pltpu.VMEM((9, 2 * heads, 1, padded), F32),
            pltpu.VMEM(conv_weight.shape, BF16),
            pltpu.VMEM((heads, conv_weight.shape[0], HEAD_DIM), F32),
            pltpu.VMEM((9, n_t, n_h), jnp.int32),
            pltpu.SMEM(clip_lengths.shape, jnp.int32),
            pltpu.SemaphoreType.DMA((4, heads)),
            pltpu.SemaphoreType.DMA((3,)),
            pltpu.SemaphoreType.DMA((4, heads)),
            pltpu.SemaphoreType.DMA((4, 9, chunks)),
            pltpu.SemaphoreType.DMA((4, 9, chunks)),
            pltpu.SemaphoreType.DMA((9,)),
            pltpu.SemaphoreType.DMA((9,)),
        ],
        compiler_params=pltpu.CompilerParams(
            collective_id=0, has_side_effects=True, vmem_limit_bytes=60 * 1024 * 1024
        ),
    )(
        query_states.reshape(flat),
        key_states.reshape(flat),
        value_states.reshape(flat),
        conv_weight,
        out_grad.reshape(flat),
        tile_mask.transpose(2, 0, 1),
        clip_lengths,
    )
    return tuple(out.reshape(query_states.shape) for out in outs)


def solution(mesh):
    tiled = P("ta", "ha", None, None)
    return jax.shard_map(
        shards,
        mesh=mesh,
        in_specs=(tiled, tiled, tiled, P(), tiled, P(), P()),
        out_specs=(tiled,) * 4,
        check_vma=False,
    )
```

time: 402 us -> 102 us (0.25)
  the two profiles are of different devices: /device:TPU:26 before, /device:TPU:25 now
where the time goes in v1:
time: 102 us
  Pallas kernels  96.7 us (95%)
  local copies, waits for them, and re-layouts  4.72 us (5%)
    pallas_call x1, Pallas kernels, shards(): pl.pallas_call(functools.partial(kernel, heads, cells, rows, padded, n_t,...  96.7 us
    unnamed x10, local copies, waits for them, and re-layouts  4.72 us

profile of v1, /device:TPU:25, one launch (start us, length us, event | category | flops | bytes accessed | tf_op | source)
XLA Modules:
  0.0 102.1 jit_solution(6609069438540365960)
XLA Ops:
  0.6 96.7 %shard_map.102 = (bf16[224,768]{1,0:T(8,128)(2,1)}, bf16[224,768]{1,0:T(8,128)(2,1)}, bf16[224,768]{1,0:T(8,128)(2,1)}, bf16[224,768]{1,0:T(8,128)(2,1)}) custom-call(bf16[224,768]{1,0:T(8,128)(2,1)} %bitcast.9, bf16[224,768]{1,0:T(8,128)(2,1)} %bitcast.10, bf16[224,768]{1,0:T(8,128)(2,1)} %bitcast.11, bf16[27,768]{1,0:T(8,128)(2,1)} %w_hbm.1, ...), custom_call_target="tpu_custom_call" | custom-call | tf_op jit(solution)/shard_map/pallas_call | solution.py:411
  97.3 0.0 copy-start.2
  97.3 1.8 %copy.15 = bf16[2,2,56,768]{3,2,1,0:T(8,128)(2,1)} copy(bf16[2,2,56,768]{3,2,1,0:T(8,128)(2,1)} %bitcast.16) | data formatting | bytes 688128
  99.1 0.0 copy-done.2
  99.1 0.0 copy-start.1
  99.1 0.7 copy.16
  99.9 0.4 copy-done.1
  100.2 0.0 copy-start
  100.2 0.7 copy.17
  101.0 0.4 copy-done
  101.3 0.7 copy.18
Async XLA Ops:
  97.3 1.8 %copy-start.2 = (bf16[224,768]{1,0:T(8,128)(2,1)S(1)}, bf16[224,768]{1,0:T(8,128)(2,1)}, u32[]{:S(2)}) copy-start(bf16[224,768]{1,0:T(8,128)(2,1)} %get-tuple-element.9) | copy-start | bytes 1032196
  99.1 1.1 %copy-start.1 = (bf16[224,768]{1,0:T(8,128)(2,1)S(1)}, bf16[224,768]{1,0:T(8,128)(2,1)}, u32[]{:S(2)}) copy-start(bf16[224,768]{1,0:T(8,128)(2,1)} %get-tuple-element.10) | copy-start | bytes 1032196
  100.2 1.1 %copy-start = (bf16[224,768]{1,0:T(8,128)(2,1)S(1)}, bf16[224,768]{1,0:T(8,128)(2,1)}, u32[]{:S(2)}) copy-start(bf16[224,768]{1,0:T(8,128)(2,1)} %get-tuple-element.11) | copy-start | bytes 1032196

commit v2 on v1

--- a/solution.py
+++ b/solution.py
@@ -18,6 +18,11 @@
 
 AK, AV, AQ, AG = 0, 1, 2, 3
 OWN, L, R, PP, PL_, PR, OO, OL, OR = range(9)
+GROUPS = ((OWN, PP), (OO,), (L, R), (PL_, PR), (OL, OR))
+KEY_GROUPS = ((OWN, PP, OO), (L, R, PL_), (PR, OL, OR))
+Y_FIRST = ((AV, 1), (AG, 1))
+FWD_UNROLL = 3
+KEY_UNROLL = 2
 
 LAST = (((1,), (1,)), ((), ()))
 
@@ -34,7 +39,7 @@
     heads, cells, rows, padded, n_t, n_h, chunks,
     q_hbm, k_hbm, v_hbm, w_hbm, g_hbm, mask_hbm, clip_hbm,
     out_hbm, dq_hbm, dk_hbm, dv_hbm,
-    tiles, probs, dprobs, slot_max, top, total, attn, delta, key_acc, value_acc, staged,
+    tiles, probs, dprobs, group_max, top, total, attn, delta, key_acc, value_acc, staged,
     bias, penalty, stat_mat, stat_out, stat_in, w_ref, wf_ref, mask_ref, clip_ref,
     load_sem, aux_sem, store_sem, send_sem, recv_sem, stat_send, stat_recv,
 ):
@@ -50,6 +55,16 @@
     h_cols = tuple(lax.rem(h + b + n_h, n_h) for b in b_cols)
     flip = (0, 2, 1)
     hpc = heads // chunks
+    has_row = (None, None, (t - a_p >= 0) & (t - a_p < n_t))
+    has_col = (None, h > 0, h < n_h - 1)
+
+    def exists(*slots):
+        found = jnp.bool_(True)
+        for slot in slots:
+            for there in (has_row[slot // 3], has_col[slot % 3]):
+                if there is not None:
+                    found = found & there
+        return found
 
     def load(arr, hd):
         src = (k_hbm, v_hbm, q_hbm, g_hbm)[arr]
@@ -59,7 +74,11 @@
             load_sem.at[arr, hd],
         )
 
-    for arr in (AK, AV, AQ, AG):
+    for chunk in range(chunks):
+        for arr in (AK, AV):
+            for hd in range(chunk * hpc, (chunk + 1) * hpc):
+                load(arr, hd).start()
+    for arr in (AQ, AG):
         for hd in range(heads):
             load(arr, hd).start()
     aux = (
@@ -72,10 +91,14 @@
 
     barrier = pltpu.get_barrier_semaphore()
     for slot in range(1, 9):
-        pl.semaphore_signal(
-            barrier, inc=1, device_id=(t_rows[slot // 3], h_cols[slot % 3]), device_id_type=MESH
-        )
-    pl.semaphore_wait(barrier, 8)
+        @pl.when(exists(slot))
+        def _():
+            pl.semaphore_signal(
+                barrier, inc=1, device_id=(t_rows[slot // 3], h_cols[slot % 3]), device_id_type=MESH
+            )
+    near_t = 2 + has_row[2].astype(jnp.int32)
+    near_h = 1 + has_col[1].astype(jnp.int32) + has_col[2].astype(jnp.int32)
+    pl.semaphore_wait(barrier, near_t * near_h - 1)
 
     def travel(arr, src_slot, to, chunk):
         row, col = src_slot // 3, src_slot % 3
@@ -103,27 +126,47 @@
 
     def send_chunk(arr, src_slot, targets, chunk):
         for to in targets:
-            copy = travel(arr, src_slot, to, chunk)
-            copy.start()
-            sent.append(copy)
+            sent.append((arr, src_slot, to, chunk))
+
+            @pl.when(exists(src_slot, to))
+            def _():
+                travel(arr, src_slot, to, chunk).start()
 
     def arrived_chunk(arr, slot, chunk):
         part = (pl.ds(chunk * hpc, hpc), pl.ds(0, rows))
         place = tiles.at[(arr, slot) + part]
-        pltpu.make_async_remote_copy(
-            src_ref=place, dst_ref=place,
-            send_sem=send_sem.at[arr, slot, chunk], recv_sem=recv_sem.at[arr, slot, chunk],
-            device_id=(t, h_cols[1]), device_id_type=MESH,
-        ).wait_recv()
+
+        @pl.when(exists(slot))
+        def _():
+            pltpu.make_async_remote_copy(
+                src_ref=place, dst_ref=place,
+                send_sem=send_sem.at[arr, slot, chunk], recv_sem=recv_sem.at[arr, slot, chunk],
+                device_id=(t_rows[1], h), device_id_type=MESH,
+            ).wait_recv()
 
     def arrived(arr, slot):
         for chunk in range(chunks):
             arrived_chunk(arr, slot, chunk)
 
-    for arr, targets in ((AK, (OO, L, R, PP)), (AV, (OO, L, R, PP)), (AQ, (L, R, PP)), (AG, (L, R, PP))):
+    for chunk in range(chunks):
+        for arr in (AK, AV):
+            for hd in range(chunk * hpc, (chunk + 1) * hpc):
+                load(arr, hd).wait()
+            send_chunk(arr, OWN, (OO, L, R, PP), chunk)
+    for arr in (AQ, AG):
         for hd in range(heads):
             load(arr, hd).wait()
-        send(arr, OWN, targets)
+        send(arr, OWN, (PP,))
+
+    def pass_sides(arr, chunk):
+        for side in (L, R):
+            arrived_chunk(arr, side, chunk)
+            send_chunk(arr, side, (PP,) if (arr, chunk) in Y_FIRST else (OO, PP), chunk)
+
+    def pass_other(arr, chunk):
+        arrived_chunk(arr, OO, chunk)
+        if (arr, chunk) in Y_FIRST:
+            send_chunk(arr, OO, (L, R), chunk)
 
     @pl.loop(0, 4 * 9)
     def _(i):
@@ -131,14 +174,17 @@
             (heads, padded - rows, HEAD_DIM), BF16
         )
 
-    @pl.loop(0, heads)
-    def _(hd):
-        zero = jnp.zeros((rows, HEAD_DIM), F32)
-        top[hd] = zero - BIG
-        total[hd] = zero
-        attn[hd] = zero
-        key_acc[hd] = zero
-        value_acc[hd] = zero
+    for slot in range(1, 9):
+        if slot != PP:
+            @pl.when(jnp.logical_not(exists(slot)))
+            def _():
+                stat_in[slot] = jnp.zeros(stat_in.shape[1:], F32)
+
+                @pl.loop(0, 4 * heads)
+                def _(i):
+                    tiles[i // heads, slot, i % heads, pl.ds(0, rows), :] = jnp.zeros(
+                        (rows, HEAD_DIM), BF16
+                    )
 
     for copy in aux:
         copy.wait()
@@ -174,43 +220,63 @@
         facing = entry(8 - index, t + a, h + b)
         penalty[slot] = jnp.where((lane < rows), jnp.where(facing > 0.5, 0.0, BIG), BIG)
 
-    def forward_slot(slot):
-        @pl.loop(0, heads)
+    def forward_group(group, chunk):
+        slots = GROUPS[group]
+
+        @pl.loop(chunk * hpc, (chunk + 1) * hpc, unroll=FWD_UNROLL)
         def _(hd):
             q = tiles[AQ, OWN, hd, pl.ds(0, rows), :]
             g = tiles[AG, OWN, hd, pl.ds(0, rows), :]
-            k = tiles[AK, slot, hd]
-            v = tiles[AV, slot, hd]
-            s = nt(q, k) + bias[slot]
-            m = jnp.max(s, axis=-1, keepdims=True)
-            p = jnp.exp2((s - m) * c2)
-            row_sum = jnp.sum(p, axis=-1, keepdims=True)
-            p_bf = p.astype(BF16)
-            probs[slot, hd] = p_bf
-            part = nn(p_bf, v)
-            dprobs[slot, hd] = nt(g, v)
+            scores = [nt(q, tiles[AK, slot, hd]) + bias[slot] for slot in slots]
+            m = jnp.max(functools.reduce(jnp.maximum, scores), axis=-1, keepdims=True)
+            ps = [jnp.exp2((s - m) * c2) for s in scores]
+            row_sum = jnp.sum(functools.reduce(jnp.add, ps), axis=-1, keepdims=True)
+            ps = [p.astype(BF16) for p in ps]
+            for slot, p in zip(slots, ps, strict=True):
+                probs[slot, hd] = p
+                dprobs[slot, hd] = nt(g, tiles[AV, slot, hd])
+            part = nn(
+                jnp.concatenate(ps, axis=1),
+                jnp.concatenate([tiles[AV, slot, hd] for slot in slots], axis=0),
+            )
             m = jnp.broadcast_to(m, (rows, HEAD_DIM))
-            slot_max[slot, hd] = m
-            old = top[hd]
-            new = jnp.maximum(old, m)
-            keep_old = jnp.exp2((old - new) * c2)
-            keep_new = jnp.exp2((m - new) * c2)
-            top[hd] = new
-            total[hd] = total[hd] * keep_old + row_sum * keep_new
-            attn[hd] = attn[hd] * keep_old + part * keep_new
-
-    def key_slot(slot):
-        @pl.loop(0, heads)
+            group_max[group, hd] = m
+            if group == 0:
+                top[hd] = m
+                total[hd] = jnp.broadcast_to(row_sum, (rows, HEAD_DIM))
+                attn[hd] = part
+            else:
+                old = top[hd]
+                new = jnp.maximum(old, m)
+                keep_old = jnp.exp2((old - new) * c2)
+                keep_new = jnp.exp2((m - new) * c2)
+                top[hd] = new
+                total[hd] = total[hd] * keep_old + row_sum * keep_new
+                attn[hd] = attn[hd] * keep_old + part * keep_new
+
+    def key_group(slots, beside=None):
+        @pl.loop(0, heads, unroll=KEY_UNROLL)
         def _(hd):
             k = tiles[AK, OWN, hd, pl.ds(0, rows), :]
             v = tiles[AV, OWN, hd, pl.ds(0, rows), :]
-            q = tiles[AQ, slot, hd]
-            g = tiles[AG, slot, hd]
-            log_total = stat_in[slot, 2 * hd] + penalty[slot]
-            p = jnp.exp2(nt(k, q) * c2 - log_total)
-            value_acc[hd] += nn(p.astype(BF16), g)
-            ds = p * (nt(v, g) - stat_in[slot, 2 * hd + 1])
-            key_acc[hd] += nn(ds.astype(BF16), q)
+            ps, dss = [], []
+            for slot in slots:
+                log_total = stat_in[slot, 2 * hd] + penalty[slot]
+                p = jnp.exp2(nt(k, tiles[AQ, slot, hd]) * c2 - log_total)
+                ps.append(p.astype(BF16))
+                ds = p * (nt(v, tiles[AG, slot, hd]) - stat_in[slot, 2 * hd + 1])
+                dss.append(ds.astype(BF16))
+            for acc, sides, arr in ((value_acc, ps, AG), (key_acc, dss, AQ)):
+                part = nn(
+                    jnp.concatenate(sides, axis=1),
+                    jnp.concatenate([tiles[arr, slot, hd] for slot in slots], axis=0),
+                )
+                if slots[0] == OWN:
+                    acc[hd] = part
+                else:
+                    acc[hd] += part
+            if beside is not None:
+                beside(hd)
 
     def convolve(arr, hd, flipped):
         r_minus, r_plus = 2 - parity, 1 + parity
@@ -263,28 +329,33 @@
     for hd in range(heads):
         wf_ref[hd] = w_ref[:, hd * HEAD_DIM:(hd + 1) * HEAD_DIM].astype(F32)
 
-    forward_slot(OWN)
     arrived(AK, PP)
     arrived(AV, PP)
-    forward_slot(PP)
-    for chunk in range(chunks):
-        for side in (L, R):
-            arrived_chunk(AK, side, chunk)
-            send_chunk(AK, side, (OO, PP), chunk)
-    arrived(AK, OO)
-    arrived(AV, OO)
-    forward_slot(OO)
-    for chunk in range(chunks):
-        for side in (L, R):
-            arrived_chunk(AV, side, chunk)
-            send_chunk(AV, side, (OO, PP), chunk)
-    send(AG, OWN, (OO,))
-    forward_slot(L)
-    forward_slot(R)
-    for slot in (PL_, PR, OL, OR):
-        arrived(AK, slot)
-        arrived(AV, slot)
-        forward_slot(slot)
+    for chunk in range(chunks):
+        forward_group(0, chunk)
+    last = chunks - 1
+    for chunk in range(chunks):
+        if chunk == last:
+            send(AQ, OWN, (L, R))
+        for arr in (AK, AV):
+            pass_sides(arr, chunk)
+        if chunk == last:
+            send(AG, OWN, (OO,))
+        else:
+            for part in range(chunks):
+                for arr in (AK, AV):
+                    pass_other(arr, part)
+                forward_group(1, part)
+        for arr in (AK, AV):
+            for slot in (PL_, PR):
+                arrived_chunk(arr, slot, chunk)
+        forward_group(2, chunk)
+        forward_group(3, chunk)
+    for chunk in range(chunks):
+        for arr in (AK, AV):
+            for slot in (OL, OR):
+                arrived_chunk(arr, slot, chunk)
+        forward_group(4, chunk)
 
     stat_mat[...] = jnp.zeros_like(stat_mat)
 
@@ -319,23 +390,25 @@
         )
 
     def stat_arrived(slot):
-        pltpu.make_async_remote_copy(
-            src_ref=stat_in.at[slot], dst_ref=stat_in.at[slot],
-            send_sem=stat_send.at[slot], recv_sem=stat_recv.at[slot],
-            device_id=(t, h_cols[1]), device_id_type=MESH,
-        ).wait_recv()
+        @pl.when(exists(slot))
+        def _():
+            pltpu.make_async_remote_copy(
+                src_ref=stat_in.at[slot], dst_ref=stat_in.at[slot],
+                send_sem=stat_send.at[slot], recv_sem=stat_recv.at[slot],
+                device_id=(t_rows[1], h), device_id_type=MESH,
+            ).wait_recv()
 
     for slot in (PP, L, R, OO, PL_, PR, OL, OR):
-        stat_travel(slot).start()
+        @pl.when(exists(slot))
+        def _():
+            stat_travel(slot).start()
 
     send(AQ, OWN, (OO,))
-    for side in (L, R):
-        for chunk in range(chunks):
-            arrived_chunk(AQ, side, chunk)
-            send_chunk(AQ, side, (OO, PP), chunk)
-    for chunk in range(chunks):
-        arrived_chunk(AG, OO, chunk)
-        send_chunk(AG, OO, (L, R), chunk)
+    send(AG, OWN, (L, R))
+    for chunk in range(chunks):
+        pass_sides(AQ, chunk)
+    for chunk in range(chunks):
+        pass_other(AG, chunk)
 
     @pl.loop(0, heads)
     def _(hd):
@@ -343,36 +416,19 @@
         d = jnp.concatenate([d, d], axis=1)
         best = top[hd]
 
-        def step(slot, acc):
-            ds = probs[slot, hd].astype(F32) * (dprobs[slot, hd] - d)
-            part = nn(ds.astype(BF16), tiles[AK, slot, hd])
-            return acc + part * jnp.exp2((slot_max[slot, hd] - best) * c2)
-
-        acc = lax.fori_loop(0, 9, step, jnp.zeros((rows, HEAD_DIM), F32))
+        acc = None
+        for group, slots in enumerate(GROUPS):
+            sides = [
+                probs[slot, hd] * (dprobs[slot, hd] - d).astype(BF16) for slot in slots
+            ]
+            part = nn(
+                jnp.concatenate(sides, axis=1),
+                jnp.concatenate([tiles[AK, slot, hd] for slot in slots], axis=0),
+            ) * jnp.exp2((group_max[group, hd] - best) * c2)
+            acc = part if acc is None else acc + part
         staged[1, hd] = (acc * (scale / total[hd])).astype(BF16)
 
     store_all(1)
-    for side in (L, R):
-        for chunk in range(chunks):
-            arrived_chunk(AG, side, chunk)
-            send_chunk(AG, side, (PP,), chunk)
-
-    @pl.loop(0, heads)
-    def _(hd):
-        pieces = convolve(AV, hd, False)
-        whole = jnp.concatenate(pieces, axis=0)
-        staged[0, hd] = (attn[hd] / total[hd] + whole).astype(BF16)
-
-    store_all(0)
-
-    key_slot(OWN)
-    for slot in (PP, L, R, PL_, PR, OO, OL, OR):
-        stat_arrived(slot)
-        if slot not in (L, R):
-            arrived(AQ, slot)
-            if slot != OO:
-                arrived(AG, slot)
-        key_slot(slot)
 
     place = lax.broadcasted_iota(jnp.int32, (rows, HEAD_DIM), 0)
     frame = (place >= 2 * cells).astype(jnp.int32)
@@ -382,21 +438,61 @@
     own_0, own_1 = frame_len(TILE_SIDE * t), frame_len(TILE_SIDE * t + 1)
     live = column < jnp.where(frame == 1, own_1, own_0)
 
-    @pl.loop(0, heads)
-    def _(hd):
+    def finish_out(hd):
+        whole = jnp.concatenate(convolve(AV, hd, False), axis=0)
+        staged[0, hd] = (attn[hd] / total[hd] + whole).astype(BF16)
+
+    def finish_grads(hd):
         whole = jnp.concatenate(convolve(AG, hd, True), axis=0)
         staged[2, hd] = jnp.where(live, key_acc[hd] * scale, 0.0).astype(BF16)
         staged[3, hd] = (jnp.where(live, value_acc[hd], 0.0) + whole).astype(BF16)
 
+    for slot in (PP, OO):
+        stat_arrived(slot)
+        arrived(AQ, slot)
+    arrived(AG, PP)
+    key_group(KEY_GROUPS[0], finish_out)
+    store_all(0)
+    for chunk in range(chunks):
+        pass_sides(AG, chunk)
+    for slot in (L, R, PL_):
+        stat_arrived(slot)
+    arrived(AQ, PL_)
+    arrived(AG, PL_)
+    key_group(KEY_GROUPS[1])
+    for slot in KEY_GROUPS[2]:
+        stat_arrived(slot)
+        arrived(AQ, slot)
+        arrived(AG, slot)
+    key_group(KEY_GROUPS[2], finish_grads)
     store_all(2)
     store_all(3)
-    for copy in sent:
-        copy.wait_send()
+    for arr, src_slot, to, chunk in sent:
+        @pl.when(exists(src_slot, to))
+        def _():
+            travel(arr, src_slot, to, chunk).wait_send()
+
     for slot in range(1, 9):
-        stat_travel(slot).wait_send()
+        @pl.when(exists(slot))
+        def _():
+            stat_travel(slot).wait_send()
+
     for which in range(4):
         for hd in range(heads):
             store(which, hd).wait()
+
+
+def hand_over(*refs):
+    ins, outs, (held, in_sem, out_sem) = refs[:4], refs[4:8], refs[8:]
+    arrive = [pltpu.make_async_copy(ins[i], held.at[i], in_sem.at[i]) for i in range(4)]
+    leave = [pltpu.make_async_copy(held.at[i], outs[i], out_sem.at[i]) for i in range(4)]
+    for copy in arrive:
+        copy.start()
+    for first, then in zip(arrive, leave, strict=True):
+        first.wait()
+        then.start()
+    for copy in leave:
+        copy.wait()
 
 
 def shards(query_states, key_states, value_states, conv_weight, out_grad, tile_mask, clip_lengths):
@@ -417,7 +513,7 @@
             pltpu.VMEM((4, 9, heads, padded, HEAD_DIM), BF16),
             pltpu.VMEM((9, heads, rows, padded), BF16),
             pltpu.VMEM((9, heads, rows, padded), F32),
-            pltpu.VMEM((9, heads, rows, HEAD_DIM), F32),
+            pltpu.VMEM((len(GROUPS), heads, rows, HEAD_DIM), F32),
             pltpu.VMEM((heads, rows, HEAD_DIM), F32),
             pltpu.VMEM((heads, rows, HEAD_DIM), F32),
             pltpu.VMEM((heads, rows, HEAD_DIM), F32),
@@ -454,6 +550,17 @@
         tile_mask.transpose(2, 0, 1),
         clip_lengths,
     )
+    outs = pl.pallas_call(
+        hand_over,
+        out_shape=[jax.ShapeDtypeStruct(flat, BF16)] * 4,
+        in_specs=[any_space] * 4,
+        out_specs=[any_space] * 4,
+        scratch_shapes=[
+            pltpu.VMEM((4,) + flat, BF16),
+            pltpu.SemaphoreType.DMA((4,)),
+            pltpu.SemaphoreType.DMA((4,)),
+        ],
+    )(*outs)
     return tuple(out.reshape(query_states.shape) for out in outs)
 
 

time: 102 us -> 66.7 us (0.65)
  the two profiles are of different devices: /device:TPU:25 before, /device:TPU:31 now
where the time goes in v2:
time: 66.7 us; the launch traced here: 66.5 us
  Pallas kernels  65.7 us (99%)
  between operations  0.8 us (1%)
    pallas_call x1, Pallas kernels, shards(): pl.pallas_call(functools.partial(kernel, heads, cells, rows, padded, n_t,...  63.5 us
    pallas_call x1, Pallas kernels, shards(): pl.pallas_call(hand_over, out_shape=[jax.ShapeDtypeStruct(flat, BF16)] *...  2.12 us

profile of v2, /device:TPU:31, one launch (start us, length us, event | category | flops | bytes accessed | tf_op | source)
XLA Modules:
  0.0 66.5 jit_solution(11574131213954834237)
XLA Ops:
  0.6 63.5 %shard_map.102 = (bf16[224,768]{1,0:T(8,128)(2,1)}, bf16[224,768]{1,0:T(8,128)(2,1)}, bf16[224,768]{1,0:T(8,128)(2,1)}, bf16[224,768]{1,0:T(8,128)(2,1)}) custom-call(bf16[224,768]{1,0:T(8,128)(2,1)} %bitcast.9, bf16[224,768]{1,0:T(8,128)(2,1)} %bitcast.10, bf16[224,768]{1,0:T(8,128)(2,1)} %bitcast.11, bf16[27,768]{1,0:T(8,128)(2,1)} %w_hbm.1, ...), custom_call_target="tpu_custom_call" | custom-call | tf_op jit(solution)/shard_map/pallas_call | solution.py:507
  64.2 2.1 %shard_map.103 = (bf16[224,768]{1,0:T(8,128)(2,1)}, bf16[224,768]{1,0:T(8,128)(2,1)}, bf16[224,768]{1,0:T(8,128)(2,1)}, bf16[224,768]{1,0:T(8,128)(2,1)}) custom-call(bf16[224,768]{1,0:T(8,128)(2,1)} %get-tuple-element.12.refs_0_, bf16[224,768]{1,0:T(8,128)(2,1)} %get-tuple-element.13.refs_1_, bf16[224,768]{1,0:T(8,128)(2,1)} %get-tuple-element.14.refs_2_, ...), custom_call_target="tpu_custom_call" | custom-call | tf_op jit(solution)/shard_map/pallas_call | solution.py:553

commit v3 on v2

--- a/solution.py
+++ b/solution.py
@@ -18,11 +18,12 @@
 
 AK, AV, AQ, AG = 0, 1, 2, 3
 OWN, L, R, PP, PL_, PR, OO, OL, OR = range(9)
-GROUPS = ((OWN, PP), (OO,), (L, R), (PL_, PR), (OL, OR))
-KEY_GROUPS = ((OWN, PP, OO), (L, R, PL_), (PR, OL, OR))
+GROUPS = ((OWN, PP), (OO,), (R, PR, OR), (L, PL_, OL))
+KEY_GROUPS = ((OWN, PP, OO), (R, PR, OR), (L, PL_, OL))
 Y_FIRST = ((AV, 1), (AG, 1))
 FWD_UNROLL = 3
-KEY_UNROLL = 2
+KEY_UNROLL = 3
+Z_CHIPS = 12
 
 LAST = (((1,), (1,)), ((), ()))
 
@@ -58,8 +59,11 @@
     has_row = (None, None, (t - a_p >= 0) & (t - a_p < n_t))
     has_col = (None, h > 0, h < n_h - 1)
 
-    def exists(*slots):
-        found = jnp.bool_(True)
+    late_left = (h > 0) & (lax.rem(h, Z_CHIPS) == 0)
+    to_early = (h < n_h - 1) & (lax.rem(h, Z_CHIPS) == Z_CHIPS - 1)
+
+    def exists(*slots, also=None):
+        found = jnp.bool_(True) if also is None else also
         for slot in slots:
             for there in (has_row[slot // 3], has_col[slot % 3]):
                 if there is not None:
@@ -112,7 +116,7 @@
         return pltpu.make_async_remote_copy(
             src_ref=tiles.at[(arr, src_slot) + part],
             dst_ref=tiles.at[(arr, dst_slot) + part],
-            send_sem=send_sem.at[arr, dst_slot, chunk],
+            send_sem=send_sem.at[arr, 0 if (src_slot, to) == (OO, R) else dst_slot, chunk],
             recv_sem=recv_sem.at[arr, dst_slot, chunk],
             device_id=device,
             device_id_type=MESH,
@@ -124,11 +128,11 @@
         for chunk in range(chunks):
             send_chunk(arr, src_slot, targets, chunk)
 
-    def send_chunk(arr, src_slot, targets, chunk):
+    def send_chunk(arr, src_slot, targets, chunk, also=None):
         for to in targets:
-            sent.append((arr, src_slot, to, chunk))
-
-            @pl.when(exists(src_slot, to))
+            sent.append((arr, src_slot, to, chunk, also))
+
+            @pl.when(exists(src_slot, to, also=also))
             def _():
                 travel(arr, src_slot, to, chunk).start()
 
@@ -158,15 +162,34 @@
             load(arr, hd).wait()
         send(arr, OWN, (PP,))
 
-    def pass_sides(arr, chunk):
-        for side in (L, R):
-            arrived_chunk(arr, side, chunk)
-            send_chunk(arr, side, (PP,) if (arr, chunk) in Y_FIRST else (OO, PP), chunk)
+    def pass_side(arr, side, chunk):
+        arrived_chunk(arr, side, chunk)
+        send_chunk(arr, side, (PP,), chunk)
+        if (arr, chunk) not in Y_FIRST:
+            send_chunk(arr, side, (OO,), chunk)
+        elif side == L:
+            send_chunk(arr, side, (OO,), chunk, late_left)
+
+    def pass_right(*parts):
+        for arr, chunk in parts:
+            pass_side(arr, R, chunk)
+
+    def pass_left(late, *parts):
+        before = len(sent)
+
+        @pl.when(late_left if late else jnp.logical_not(late_left))
+        def _():
+            for arr, chunk in parts:
+                pass_side(arr, L, chunk)
+
+        if late:
+            del sent[before:]
 
     def pass_other(arr, chunk):
         arrived_chunk(arr, OO, chunk)
         if (arr, chunk) in Y_FIRST:
-            send_chunk(arr, OO, (L, R), chunk)
+            send_chunk(arr, OO, (L,), chunk)
+            send_chunk(arr, OO, (R,), chunk, jnp.logical_not(to_early))
 
     @pl.loop(0, 4 * 9)
     def _(i):
@@ -254,8 +277,8 @@
                 total[hd] = total[hd] * keep_old + row_sum * keep_new
                 attn[hd] = attn[hd] * keep_old + part * keep_new
 
-    def key_group(slots, beside=None):
-        @pl.loop(0, heads, unroll=KEY_UNROLL)
+    def key_group(slots, chunk, beside=None):
+        @pl.loop(chunk * hpc, (chunk + 1) * hpc, unroll=KEY_UNROLL)
         def _(hd):
             k = tiles[AK, OWN, hd, pl.ds(0, rows), :]
             v = tiles[AV, OWN, hd, pl.ds(0, rows), :]
@@ -333,29 +356,39 @@
     arrived(AV, PP)
     for chunk in range(chunks):
         forward_group(0, chunk)
-    last = chunks - 1
+    first, second = ((AK, 0), (AV, 0)), ((AK, 1), (AV, 1))
+    pass_right(*first)
+    pass_left(False, *first)
+    for arr, chunk in first:
+        pass_other(arr, chunk)
+    forward_group(1, 0)
+    for arr, chunk in second:
+        pass_other(arr, chunk)
     for chunk in range(chunks):
-        if chunk == last:
-            send(AQ, OWN, (L, R))
-        for arr in (AK, AV):
-            pass_sides(arr, chunk)
-        if chunk == last:
-            send(AG, OWN, (OO,))
-        else:
-            for part in range(chunks):
-                for arr in (AK, AV):
-                    pass_other(arr, part)
-                forward_group(1, part)
-        for arr in (AK, AV):
-            for slot in (PL_, PR):
+        for arr in (AQ, AG):
+            send_chunk(arr, OWN, (L, R), chunk)
+    forward_group(1, 1)
+
+    def arrived_all(arrs, slots, chunk):
+        for slot in slots:
+            for arr in arrs:
                 arrived_chunk(arr, slot, chunk)
-        forward_group(2, chunk)
-        forward_group(3, chunk)
+
+    arrived_all((AK, AV), (PR, OR), 0)
+    forward_group(2, 0)
+    pass_right(*second)
+    pass_left(False, *second)
     for chunk in range(chunks):
-        for arr in (AK, AV):
-            for slot in (OL, OR):
-                arrived_chunk(arr, slot, chunk)
-        forward_group(4, chunk)
+        for arr in (AQ, AG):
+            send_chunk(arr, OWN, (OO,), chunk)
+    arrived_all((AK, AV), (PR, OR), 1)
+    forward_group(2, 1)
+    pass_left(True, *first, second[0])
+    arrived_all((AK, AV), (PL_, OL), 0)
+    forward_group(3, 0)
+    pass_left(True, second[1])
+    arrived_all((AK, AV), (PL_, OL), 1)
+    forward_group(3, 1)
 
     stat_mat[...] = jnp.zeros_like(stat_mat)
 
@@ -403,12 +436,12 @@
         def _():
             stat_travel(slot).start()
 
-    send(AQ, OWN, (OO,))
-    send(AG, OWN, (L, R))
-    for chunk in range(chunks):
-        pass_sides(AQ, chunk)
+    for arr in (AQ, AG):
+        pass_right((arr, 0))
+        pass_left(False, (arr, 0))
     for chunk in range(chunks):
         pass_other(AG, chunk)
+    pass_left(True, (AQ, 0))
 
     @pl.loop(0, heads)
     def _(hd):
@@ -447,28 +480,33 @@
         staged[2, hd] = jnp.where(live, key_acc[hd] * scale, 0.0).astype(BF16)
         staged[3, hd] = (jnp.where(live, value_acc[hd], 0.0) + whole).astype(BF16)
 
+    pass_left(True, (AG, 0))
+    pass_right((AQ, 1))
+    pass_left(False, (AQ, 1))
     for slot in (PP, OO):
         stat_arrived(slot)
-        arrived(AQ, slot)
-    arrived(AG, PP)
-    key_group(KEY_GROUPS[0], finish_out)
+    arrived_all((AQ, AG), (PP,), 0)
+    arrived_all((AQ,), (OO,), 0)
+    key_group(KEY_GROUPS[0], 0, finish_out)
+    pass_left(True, (AQ, 1))
+    pass_right((AG, 1))
+    pass_left(False, (AG, 1))
+    arrived_all((AQ, AG), (PP,), 1)
+    arrived_all((AQ,), (OO,), 1)
+    key_group(KEY_GROUPS[0], 1, finish_out)
     store_all(0)
-    for chunk in range(chunks):
-        pass_sides(AG, chunk)
-    for slot in (L, R, PL_):
-        stat_arrived(slot)
-    arrived(AQ, PL_)
-    arrived(AG, PL_)
-    key_group(KEY_GROUPS[1])
-    for slot in KEY_GROUPS[2]:
-        stat_arrived(slot)
-        arrived(AQ, slot)
-        arrived(AG, slot)
-    key_group(KEY_GROUPS[2], finish_grads)
+    pass_left(True, (AG, 1))
+    for group, beside in ((1, None), (2, finish_grads)):
+        slots = KEY_GROUPS[group]
+        for slot in slots:
+            stat_arrived(slot)
+        for chunk in range(chunks):
+            arrived_all((AQ, AG), slots[1:], chunk)
+            key_group(slots, chunk, beside)
     store_all(2)
     store_all(3)
-    for arr, src_slot, to, chunk in sent:
-        @pl.when(exists(src_slot, to))
+    for arr, src_slot, to, chunk, also in sent:
+        @pl.when(exists(src_slot, to, also=also))
         def _():
             travel(arr, src_slot, to, chunk).wait_send()
 

time: 66.7 us -> 78.8 us (1.18)
  Pallas kernels: 65.7 us -> 77.8 us
    pallas_call x1, Pallas kernels: 63.5 us -> 75.6 us  [shards(): pl.pallas_call(functools.partial(kernel, heads, cells, rows, padded, n_t,...]
where the time goes in v3:
time: 78.8 us; the launch traced here: 78.6 us
  Pallas kernels  77.8 us (99%)
  between operations  0.8 us (1%)
    pallas_call x1, Pallas kernels, shards(): pl.pallas_call(functools.partial(kernel, heads, cells, rows, padded, n_t,...  75.6 us
    pallas_call x1, Pallas kernels, shards(): pl.pallas_call(hand_over, out_shape=[jax.ShapeDtypeStruct(flat, BF16)] *...  2.12 us

profile of v3, /device:TPU:31, one launch (start us, length us, event | category | flops | bytes accessed | tf_op | source)
XLA Modules:
  0.0 78.6 jit_solution(3685069858047630494)
XLA Ops:
  0.6 75.6 %shard_map.102 = (bf16[224,768]{1,0:T(8,128)(2,1)}, bf16[224,768]{1,0:T(8,128)(2,1)}, bf16[224,768]{1,0:T(8,128)(2,1)}, bf16[224,768]{1,0:T(8,128)(2,1)}) custom-call(bf16[224,768]{1,0:T(8,128)(2,1)} %bitcast.9, bf16[224,768]{1,0:T(8,128)(2,1)} %bitcast.10, bf16[224,768]{1,0:T(8,128)(2,1)} %bitcast.11, bf16[27,768]{1,0:T(8,128)(2,1)} %w_hbm.1, ...), custom_call_target="tpu_custom_call" | custom-call | tf_op jit(solution)/shard_map/pallas_call | solution.py:545
  76.3 2.1 %shard_map.103 = (bf16[224,768]{1,0:T(8,128)(2,1)}, bf16[224,768]{1,0:T(8,128)(2,1)}, bf16[224,768]{1,0:T(8,128)(2,1)}, bf16[224,768]{1,0:T(8,128)(2,1)}) custom-call(bf16[224,768]{1,0:T(8,128)(2,1)} %get-tuple-element.12.refs_0_, bf16[224,768]{1,0:T(8,128)(2,1)} %get-tuple-element.13.refs_1_, bf16[224,768]{1,0:T(8,128)(2,1)} %get-tuple-element.14.refs_2_, ...), custom_call_target="tpu_custom_call" | custom-call | tf_op jit(solution)/shard_map/pallas_call | solution.py:591

commit v4 on v3

--- a/solution.py
+++ b/solution.py
@@ -42,7 +42,7 @@
     out_hbm, dq_hbm, dk_hbm, dv_hbm,
     tiles, probs, dprobs, group_max, top, total, attn, delta, key_acc, value_acc, staged,
     bias, penalty, stat_mat, stat_out, stat_in, w_ref, wf_ref, mask_ref, clip_ref,
-    load_sem, aux_sem, store_sem, send_sem, recv_sem, stat_send, stat_recv,
+    late_sem, load_sem, aux_sem, store_sem, send_sem, recv_sem, stat_send, stat_recv,
 ):
     scale = HEAD_DIM ** -0.5
     c2 = scale * LOG2E
@@ -95,14 +95,21 @@
 
     barrier = pltpu.get_barrier_semaphore()
     for slot in range(1, 9):
-        @pl.when(exists(slot))
+        @pl.when(exists(slot, also=jnp.logical_not(to_early) if slot % 3 == R else None))
         def _():
             pl.semaphore_signal(
                 barrier, inc=1, device_id=(t_rows[slot // 3], h_cols[slot % 3]), device_id_type=MESH
             )
     near_t = 2 + has_row[2].astype(jnp.int32)
-    near_h = 1 + has_col[1].astype(jnp.int32) + has_col[2].astype(jnp.int32)
+    here_left = has_col[1] & jnp.logical_not(late_left)
+    near_h = 1 + here_left.astype(jnp.int32) + has_col[2].astype(jnp.int32)
     pl.semaphore_wait(barrier, near_t * near_h - 1)
+    for slot in (R, PR, OR):
+        @pl.when(exists(slot, also=to_early))
+        def _():
+            pl.semaphore_signal(
+                late_sem, inc=1, device_id=(t_rows[slot // 3], h_cols[slot % 3]), device_id_type=MESH
+            )
 
     def travel(arr, src_slot, to, chunk):
         row, col = src_slot // 3, src_slot % 3
@@ -116,7 +123,7 @@
         return pltpu.make_async_remote_copy(
             src_ref=tiles.at[(arr, src_slot) + part],
             dst_ref=tiles.at[(arr, dst_slot) + part],
-            send_sem=send_sem.at[arr, 0 if (src_slot, to) == (OO, R) else dst_slot, chunk],
+            send_sem=send_sem.at[arr, {(OO, L): 9, (OO, R): 0}.get((src_slot, to), dst_slot), chunk],
             recv_sem=recv_sem.at[arr, dst_slot, chunk],
             device_id=device,
             device_id_type=MESH,
@@ -156,7 +163,8 @@
         for arr in (AK, AV):
             for hd in range(chunk * hpc, (chunk + 1) * hpc):
                 load(arr, hd).wait()
-            send_chunk(arr, OWN, (OO, L, R, PP), chunk)
+            send_chunk(arr, OWN, (OO, R, PP), chunk)
+            send_chunk(arr, OWN, (L,), chunk, jnp.logical_not(late_left))
     for arr in (AQ, AG):
         for hd in range(heads):
             load(arr, hd).wait()
@@ -167,29 +175,20 @@
         send_chunk(arr, side, (PP,), chunk)
         if (arr, chunk) not in Y_FIRST:
             send_chunk(arr, side, (OO,), chunk)
-        elif side == L:
-            send_chunk(arr, side, (OO,), chunk, late_left)
 
     def pass_right(*parts):
         for arr, chunk in parts:
             pass_side(arr, R, chunk)
 
-    def pass_left(late, *parts):
-        before = len(sent)
-
-        @pl.when(late_left if late else jnp.logical_not(late_left))
-        def _():
-            for arr, chunk in parts:
-                pass_side(arr, L, chunk)
-
-        if late:
-            del sent[before:]
+    def pass_left(*parts):
+        for arr, chunk in parts:
+            pass_side(arr, L, chunk)
 
     def pass_other(arr, chunk):
         arrived_chunk(arr, OO, chunk)
         if (arr, chunk) in Y_FIRST:
             send_chunk(arr, OO, (L,), chunk)
-            send_chunk(arr, OO, (R,), chunk, jnp.logical_not(to_early))
+            send_chunk(arr, OO, (R,), chunk)
 
     @pl.loop(0, 4 * 9)
     def _(i):
@@ -358,10 +357,17 @@
         forward_group(0, chunk)
     first, second = ((AK, 0), (AV, 0)), ((AK, 1), (AV, 1))
     pass_right(*first)
-    pass_left(False, *first)
+    @pl.when(late_left)
+    def _():
+        pl.semaphore_wait(late_sem, near_t)
+
+    for arr, chunk in first + second:
+        send_chunk(arr, OWN, (L,), chunk, late_left)
+    pass_left(*first)
     for arr, chunk in first:
         pass_other(arr, chunk)
     forward_group(1, 0)
+
     for arr, chunk in second:
         pass_other(arr, chunk)
     for chunk in range(chunks):
@@ -377,16 +383,14 @@
     arrived_all((AK, AV), (PR, OR), 0)
     forward_group(2, 0)
     pass_right(*second)
-    pass_left(False, *second)
+    pass_left(*second)
     for chunk in range(chunks):
         for arr in (AQ, AG):
             send_chunk(arr, OWN, (OO,), chunk)
     arrived_all((AK, AV), (PR, OR), 1)
     forward_group(2, 1)
-    pass_left(True, *first, second[0])
     arrived_all((AK, AV), (PL_, OL), 0)
     forward_group(3, 0)
-    pass_left(True, second[1])
     arrived_all((AK, AV), (PL_, OL), 1)
     forward_group(3, 1)
 
@@ -438,10 +442,9 @@
 
     for arr in (AQ, AG):
         pass_right((arr, 0))
-        pass_left(False, (arr, 0))
+        pass_left((arr, 0))
     for chunk in range(chunks):
         pass_other(AG, chunk)
-    pass_left(True, (AQ, 0))
 
     @pl.loop(0, heads)
     def _(hd):
@@ -480,22 +483,19 @@
         staged[2, hd] = jnp.where(live, key_acc[hd] * scale, 0.0).astype(BF16)
         staged[3, hd] = (jnp.where(live, value_acc[hd], 0.0) + whole).astype(BF16)
 
-    pass_left(True, (AG, 0))
     pass_right((AQ, 1))
-    pass_left(False, (AQ, 1))
+    pass_left((AQ, 1))
     for slot in (PP, OO):
         stat_arrived(slot)
     arrived_all((AQ, AG), (PP,), 0)
     arrived_all((AQ,), (OO,), 0)
     key_group(KEY_GROUPS[0], 0, finish_out)
-    pass_left(True, (AQ, 1))
     pass_right((AG, 1))
-    pass_left(False, (AG, 1))
+    pass_left((AG, 1))
     arrived_all((AQ, AG), (PP,), 1)
     arrived_all((AQ,), (OO,), 1)
     key_group(KEY_GROUPS[0], 1, finish_out)
     store_all(0)
-    pass_left(True, (AG, 1))
     for group, beside in ((1, None), (2, finish_grads)):
         slots = KEY_GROUPS[group]
         for slot in slots:
@@ -568,10 +568,11 @@
             pltpu.VMEM((heads, conv_weight.shape[0], HEAD_DIM), F32),
             pltpu.VMEM((9, n_t, n_h), jnp.int32),
             pltpu.SMEM(clip_lengths.shape, jnp.int32),
+            pltpu.SemaphoreType.REGULAR,
             pltpu.SemaphoreType.DMA((4, heads)),
             pltpu.SemaphoreType.DMA((3,)),
             pltpu.SemaphoreType.DMA((4, heads)),
-            pltpu.SemaphoreType.DMA((4, 9, chunks)),
+            pltpu.SemaphoreType.DMA((4, 10, chunks)),
             pltpu.SemaphoreType.DMA((4, 9, chunks)),
             pltpu.SemaphoreType.DMA((9,)),
             pltpu.SemaphoreType.DMA((9,)),

time: 78.8 us -> 64.5 us (0.82)
  the two profiles are of different devices: /device:TPU:31 before, /device:TPU:38 now
where the time goes in v4:
time: 64.5 us; the launch traced here: 64.3 us
  Pallas kernels  63.5 us (98%)
  between operations  0.8 us (1%)
    pallas_call x1, Pallas kernels, shards(): pl.pallas_call(functools.partial(kernel, heads, cells, rows, padded, n_t,...  61.4 us
    pallas_call x1, Pallas kernels, shards(): pl.pallas_call(hand_over, out_shape=[jax.ShapeDtypeStruct(flat, BF16)] *...  2.12 us

profile of v4, /device:TPU:38, one launch (start us, length us, event | category | flops | bytes accessed | tf_op | source)
XLA Modules:
  0.0 64.3 jit_solution(6248825239971916928)
XLA Ops:
  0.6 61.4 %shard_map.102 = (bf16[224,768]{1,0:T(8,128)(2,1)}, bf16[224,768]{1,0:T(8,128)(2,1)}, bf16[224,768]{1,0:T(8,128)(2,1)}, bf16[224,768]{1,0:T(8,128)(2,1)}) custom-call(bf16[224,768]{1,0:T(8,128)(2,1)} %bitcast.9, bf16[224,768]{1,0:T(8,128)(2,1)} %bitcast.10, bf16[224,768]{1,0:T(8,128)(2,1)} %bitcast.11, bf16[27,768]{1,0:T(8,128)(2,1)} %w_hbm.1, ...), custom_call_target="tpu_custom_call" | custom-call | tf_op jit(solution)/shard_map/pallas_call | solution.py:545
  62.0 2.1 %shard_map.103 = (bf16[224,768]{1,0:T(8,128)(2,1)}, bf16[224,768]{1,0:T(8,128)(2,1)}, bf16[224,768]{1,0:T(8,128)(2,1)}, bf16[224,768]{1,0:T(8,128)(2,1)}) custom-call(bf16[224,768]{1,0:T(8,128)(2,1)} %get-tuple-element.12.refs_0_, bf16[224,768]{1,0:T(8,128)(2,1)} %get-tuple-element.13.refs_1_, bf16[224,768]{1,0:T(8,128)(2,1)} %get-tuple-element.14.refs_2_, ...), custom_call_target="tpu_custom_call" | custom-call | tf_op jit(solution)/shard_map/pallas_call | solution.py:592
